TPU v7x, 32 devices: a whole 2x2x4 slice. The times are simulated.
32 devices in a mesh: dp: 8 (over y, x, core), tensor: 4 (over z).
Axes of the slice: x: 2, y: 2, z: 4, core: 2. Of those that a mesh axis runs over, the one named last changes fastest.
Arguments:
- block_in: bfloat16 [2048, 1024], P('dp'), may hold values from -6 to 6
- first_values: bfloat16 [2048, 1024], P('dp', 'tensor'), may hold values from -6 to 6
- cotangent: bfloat16 [2048, 1024], P('dp'), may hold values from -6 to 6
- shared_vectors: float32 [11, 1024], replicated, may hold values from -0.5 to 1.5, as said below
- head_vectors: float32 [8, 1024], P(None, 'tensor'), may hold values from -7.5 to 1.5, as said below
- projections: bfloat16 [3, 1024, 1024], P(None, None, 'tensor'), may hold values from -0.1875 to 0.1875
- reducers: bfloat16 [1024, 288], replicated, may hold values from -0.1875 to 0.1875
- expanders: bfloat16 [288, 1024], P(None, 'tensor'), may hold values from -1 to 1
- readout: bfloat16 [1024, 1024], P('tensor'), may hold values from -0.1875 to 0.1875
- widener: bfloat16 [1024, 4096], P(None, 'tensor'), may hold values from -0.1875 to 0.1875
- narrower: bfloat16 [4096, 1024], P('tensor'), may hold values from -0.09375 to 0.09375
Outputs:
- block_out: bfloat16 [2048, 1024], P('dp')
- grad_input: float32 [2048, 1024], P('dp')
- grad_first: float32 [2048, 1024], P('dp', 'tensor')
- grad_shared: float32 [11, 1024], replicated
- grad_head: float32 [8, 1024], P(None, 'tensor')
- grad_projections: float32 [3, 1024, 1024], P(None, 'dp', 'tensor')
- grad_reducers: float32 [1024, 288], P('dp')
- grad_expanders: float32 [288, 1024], P(None, 'tensor')
- grad_readout: float32 [1024, 1024], P('tensor', 'dp')
- grad_widener: float32 [1024, 4096], P('dp', 'tensor')
- grad_narrower: float32 [4096, 1024], P('tensor', 'dp')
Inputs may be any that keep to these rules, and one draw needn't show every extreme that they name: `head_vectors`: row 0 holds decay offsets, row 1 rate offsets, row 2 value-residual offsets, row 3 key-normalization scales, row 4 key-rate mixing, row 5 bonus weights, rows 6 and 7 the group norm's gain and bias. `shared_vectors`: rows 0 and 1 are the first norm's gain and bias, rows 2 to 7 the token-shift mixing of receptance, decay, key, value, rate and gate, rows 8 and 9 the second norm's gain and bias, row 10 the channel-mix shift mixing.
All inputs are finite; a program needn't handle non-finite values.
Results may differ from a plain program's by a relative error of at most 0.011.
Values sent between devices are 32-bit elements; how exact they have to be, the bound alone decides.
No kernel may reach another device: no remote copies, remote signals or barrier semaphores. Data moves between devices by JAX's collectives and lax.ppermute only.
A program may use at most 128 MiB of HBM per device.

v0:
```python
import functools

import jax
import jax.numpy as jnp
from jax import lax
from jax.experimental import pallas as pl
from jax.experimental.pallas import tpu as pltpu
from jax.sharding import PartitionSpec as P

HEAD = 64
RANK_W = 64
RANK_A = 64
RANK_V = 32
CH = 64
F32 = jnp.float32
BF16 = jnp.bfloat16
NN = (((1,), (0,)), ((), ()))
NT = (((1,), (1,)), ((), ()))
TN = (((0,), (0,)), ((), ()))


def halves(x):
    high = x.astype(BF16)
    return high, (x - high.astype(F32)).astype(BF16)


def raw(a, b, dims):
    return lax.dot_general(a, b, dims, preferred_element_type=F32)


def pair(x):
    return x if isinstance(x, tuple) else halves(x)


def product(a, b, dims):
    (ah, al), (bh, bl) = pair(a), pair(b)
    return raw(ah, bh, dims) + (raw(ah, bl, dims) + raw(al, bh, dims))


def masked(x, mask):
    return tuple(part * mask for part in pair(x))


def beside(parts, axis):
    return tuple(jnp.concatenate(p, axis=axis) for p in zip(*(pair(x) for x in parts)))


def with_ones(ones, x, dims=NN):
    high = x.astype(BF16)
    rest = x - high.astype(F32)
    mid = rest.astype(BF16)
    low = (rest - mid.astype(F32)).astype(BF16)
    return raw(ones, high, dims) + (raw(ones, mid, dims) + raw(ones, low, dims))


class Grid:
    def __init__(self, tokens, lanes):
        self.tokens, self.lanes = tokens, lanes
        self.heads = lanes // HEAD
        self.blocks = tokens // CH
        row = lax.broadcasted_iota(jnp.int32, (tokens, tokens), 0)
        col = lax.broadcasted_iota(jnp.int32, (tokens, tokens), 1)
        same = (row // CH) == (col // CH)
        self.row, self.col, self.same = row, col, same
        self.strict = (same & (row > col)).astype(F32)
        self.incl = (same & (row >= col)).astype(F32)
        self.strict_up = (same & (row < col)).astype(F32)
        self.incl_up = (same & (row <= col)).astype(F32)
        self.eye = (row == col).astype(F32)
        lrow = lax.broadcasted_iota(jnp.int32, (lanes, lanes), 0)
        lcol = lax.broadcasted_iota(jnp.int32, (lanes, lanes), 1)
        self.block = ((lrow // HEAD) == (lcol // HEAD)).astype(F32)
        self.lane = lax.broadcasted_iota(jnp.int32, (1, lanes), 1) // HEAD

    def mask(self, h):
        return (self.lane == h).astype(F32).astype(BF16)

    def each(self, body):
        def step(h, carry):
            body(h, self.mask(h))
            return carry

        lax.fori_loop(0, self.heads, step, 0)

    def seg(self, x):
        high, low = halves(x)
        ones = self.block.astype(BF16)
        return raw(high, ones, NN) + raw(low, ones, NN)

    def off(self, level):
        return (
            ((self.row >> (level + 1)) == (self.col >> (level + 1)))
            & ((self.row >> level) > (self.col >> level))
        ).astype(F32)


def prepare(g, r, k, vr, first, dlin, rlin, vlin, hv):
    p = [hv[i : i + 1, :] for i in range(8)]
    gone = lax.logistic(p[0] + dlin)
    dlog = gone * (-0.6065306597126334)
    rate = lax.logistic(p[1] + rlin)
    sv = lax.logistic(p[2] + vlin)
    value = vr + (first - vr) * sv
    y = k * p[3]
    inv = lax.rsqrt(g.seg(y * y) + 1e-6)
    direction = y * inv
    keys = k * (1.0 + (rate - 1.0) * p[4])
    cumul = with_ones(g.incl.astype(BF16), dlog)
    before = cumul - dlog
    up = jnp.exp(cumul)
    upb = jnp.exp(before)
    down = jnp.exp(-cumul)
    finals = [jnp.exp(cumul[(c + 1) * CH - 1 : (c + 1) * CH, :]) for c in range(g.blocks)]
    last = jnp.concatenate([jnp.broadcast_to(f, (CH, g.lanes)) for f in finals], axis=0)
    ins = direction * rate
    Q = r * up
    R = -direction * upb
    I = ins * down
    K = keys * down
    return dict(p=p, gone=gone, dlog=dlog, rate=rate, sv=sv, value=value, inv=inv,
                direction=direction, keys=keys, up=up, upb=upb, down=down, finals=finals,
                last=last, Q=Q, R=R, I=I, K=K, Ie=I * last, Ke=K * last)


def forward_math(g, r, k, vr, first, dlin, rlin, vlin, hv, t, u, out, a, w):
    d = prepare(g, r, k, vr, first, dlin, rlin, vlin, hv)
    Q, R, I, K, Ie, Ke, V = (d[n] for n in ("Q", "R", "I", "K", "Ie", "Ke", "value"))
    Qp, Rp, Ip, Kp, Vp = (halves(x) for x in (Q, R, I, K, V))

    def open_head(h, m):
        full = product(masked(Rp, m), Ip, NT) * g.strict
        a[h] = full
        t[h] = g.eye + full * g.off(0)

    g.each(open_head)

    def level(n, carry):
        off = g.off(n)
        mats = [halves(t[h]) for h in range(g.heads)]
        mids = [product(a[h] * off, mats[h], NN) for h in range(g.heads)]
        for h in range(g.heads):
            t[h] = t[h] + product(mats[h], mids[h], NN)
        return carry

    lax.fori_loop(1, CH.bit_length() - 1, level, 0)
    w[...] = jnp.zeros_like(R)
    u[...] = jnp.zeros_like(R)

    def solve_head(h, m):
        solved = halves(t[h])
        right = product(product(masked(Rp, m), Kp, NT) * g.strict, masked(Vp, m), NN)
        w[...] += product(solved, masked(Rp, m), NN)
        u[...] += product(solved, right, NN)

    g.each(solve_head)
    state = jnp.zeros((g.lanes, g.lanes), F32)
    states = []
    for c in range(g.blocks):
        s = slice(c * CH, (c + 1) * CH)
        states.append(state)
        if c:
            both = product(jnp.concatenate([w[s], Q[s]], axis=0), state, NT)
            u[s] = u[s] + both[:CH]
            out[s] = both[CH:]
        else:
            out[s] = jnp.zeros((CH, g.lanes), F32)
        if c < g.blocks - 1:
            add = product(jnp.concatenate([u[s], V[s]], axis=0), jnp.concatenate([Ie[s], Ke[s]], axis=0), TN)
            state = state * d["finals"][c] + add * g.block
    Up = halves(u[...])

    def close_head(h, m):
        mine = masked(Qp, m)
        mats = [product(mine, x, NT) * g.incl for x in (Ip, Kp)]
        out[...] += product(beside(mats, 1), beside([masked(Up, m), masked(Vp, m)], 0), NN)

    g.each(close_head)
    return d, states


def tail(g, d, r, mixed):
    p = d["p"]
    centred = mixed - g.seg(mixed) * (1.0 / HEAD)
    spread = lax.rsqrt(g.seg(centred * centred) * (1.0 / HEAD) + 0.00064)
    unit = centred * spread
    reward = g.seg(r * d["keys"] * p[5])
    whole = unit * p[6] + p[7] + reward * d["value"]
    return unit, spread, reward, whole


def rowsum(x):
    return jnp.sum(x, axis=0, keepdims=True)


def backward_math(g, r, k, vr, first, dlin, rlin, vlin, glin, hv, t, U, states, mixed, d_core, x_acc, z_acc, v_acc, q_acc, r_acc, i_acc, k_acc):
    d = prepare(g, r, k, vr, first, dlin, rlin, vlin, hv)
    p = d["p"]
    unit, spread, reward, whole = tail(g, d, r, mixed)
    keys, V, rate, direction, sv = d["keys"], d["value"], d["rate"], d["direction"], d["sv"]
    d_glin = d_core * whole
    dP = d_core * glin
    h7 = rowsum(dP)
    h6 = rowsum(dP * unit)
    dn = dP * p[6]
    dO = spread * (dn - g.seg(dn) * (1.0 / HEAD) - unit * (g.seg(dn * unit) * (1.0 / HEAD)))
    d_reward = g.seg(dP * V)
    h5 = rowsum(d_reward * r * keys)
    dV = dP * reward
    dr = d_reward * keys * p[5]
    dkeys = d_reward * r * p[5]

    Q, R, I, K, Ie, Ke = (d[n] for n in ("Q", "R", "I", "K", "Ie", "Ke"))
    Qp, Rp, Ip, Kp, Vp, Up, Op, Ep = (halves(x) for x in (Q, R, I, K, V, U, dO, Ie))
    x_acc[...] = jnp.zeros_like(Q)
    z_acc[...] = jnp.zeros_like(Q)

    def open_head(h, m):
        solved = halves(t[h])
        mid = product(product(masked(Ip, m), Qp, NT) * g.incl_up, masked(Op, m), NN)
        x_acc[...] += product(solved, mid, TN)
        z_acc[...] += product(solved, masked(Ep, m), TN)

    g.each(open_head)
    dX0, Z = x_acc, z_acc
    grad = jnp.zeros((g.lanes, g.lanes), F32)
    dXs, dVs, dIes, dKes, dfs, dQs, dRs = ([None] * g.blocks for _ in range(7))
    for c in reversed(range(g.blocks)):
        s = slice(c * CH, (c + 1) * CH)
        if c < g.blocks - 1:
            out = product(jnp.concatenate([Z[s], Ke[s]], axis=0), grad, NT)
            dX = dX0[s] + out[:CH]
            dVs[c] = out[CH:]
            out = product(jnp.concatenate([U[s], V[s]], axis=0), grad, NN)
            dIes[c] = out[:CH]
            dKes[c] = out[CH:]
            dfs[c] = rowsum(states[c] * grad) * d["finals"][c]
        else:
            dX = dX0[s]
            zero = jnp.zeros((CH, g.lanes), F32)
            dVs[c], dIes[c], dKes[c], dfs[c] = zero, zero, zero, zero[:1]
        dXs[c] = dX
        if c:
            out = product(jnp.concatenate([dO[s], dX], axis=0), states[c], NN)
            dQs[c], dRs[c] = out[:CH], out[CH:]
            add = product(jnp.concatenate([dO[s], dX], axis=0), jnp.concatenate([Q[s], R[s]], axis=0), TN)
            grad = grad * d["finals"][c] + add * g.block
        else:
            dQs[c], dRs[c] = jnp.zeros((CH, g.lanes), F32), jnp.zeros((CH, g.lanes), F32)
    join = functools.partial(jnp.concatenate, axis=0)
    dX, dIe, dKe = join(dXs), join(dIes), join(dKes)
    v_acc[...] = dV + join(dVs)
    q_acc[...] = join(dQs)
    r_acc[...] = join(dRs)
    i_acc[...] = jnp.zeros_like(Q)
    k_acc[...] = jnp.zeros_like(Q)
    Xp = halves(dX)

    def close_head(h, m):
        Qm, Rm, Im, Km, Vm, Um, Om, Xm = (masked(x, m) for x in (Qp, Rp, Ip, Kp, Vp, Up, Op, Xp))

        def both(x, y, first, second, up):
            mats = [product(x, p, NT) * mask for p, mask in zip(y, up)]
            return product(beside(mats, 1), beside([first, second], 0), NN)

        low, high = (g.incl, g.incl), (g.strict_up, g.incl_up)
        v_acc[...] += both(Km, (Rp, Qp), Xm, Om, high)
        q_acc[...] += both(Om, (Up, Vp), Im, Km, low)
        r_acc[...] += both(Xm, (Up, Vp), Im, Km, (g.strict, g.strict))
        i_acc[...] += both(Um, (Xp, Op), Rm, Qm, high)
        k_acc[...] += both(Vm, (Xp, Op), Rm, Qm, high)

    g.each(close_head)
    dV, dQ, dR, dI, dK = (ref[...] for ref in (v_acc, q_acc, r_acc, i_acc, k_acc))

    dr = dr + dQ * d["up"]
    before = dR * R
    ends = dIe * Ie + dKe * Ke
    dcumul = dQ * Q + before - dI * I - dK * K - ends
    ddlog = with_ones(g.incl_up.astype(BF16), dcumul) - before
    tails = []
    for c in range(g.blocks):
        s = slice(c * CH, (c + 1) * CH)
        tails.append(jnp.broadcast_to(rowsum(ends[s]) + dfs[c], (CH, g.lanes)))
    ddlog = ddlog + join(tails)
    drem = dR * d["upb"]
    dins = (dI + dIe * d["last"]) * d["down"]
    dkeys = dkeys + (dK + dKe * d["last"]) * d["down"]

    ddir = dins * rate - drem
    drate = dins * direction + dkeys * k * p[4]
    h4 = rowsum(dkeys * k * (rate - 1.0))
    dk = dkeys * (1.0 + (rate - 1.0) * p[4])
    dy = d["inv"] * (ddir - direction * g.seg(ddir * direction))
    dk = dk + dy * p[3]
    h3 = rowsum(dy * k)
    d_first = dV * sv
    dvr = dV - d_first
    d_vlin = dV * (first - vr) * sv * (1.0 - sv)
    d_rlin = drate * rate * (1.0 - rate)
    d_dlin = ddlog * d["dlog"] * (1.0 - d["gone"])
    heads = [rowsum(d_dlin), rowsum(d_rlin), rowsum(d_vlin), h3, h4, h5, h6, h7]
    return dr, dk, dvr, d_first, d_dlin, d_rlin, d_vlin, d_glin, jnp.concatenate(heads, axis=0)


def segment(lanes):
    lane = lax.broadcasted_iota(jnp.int32, (1, lanes), 1)
    cuts = (RANK_W, RANK_W + RANK_A, RANK_W + RANK_A + RANK_V)
    return sum((lane >= c).astype(jnp.int32) for c in cuts)


def layer_norm(rows, gain, offset):
    centred = rows - jnp.mean(rows, axis=-1, keepdims=True)
    scale = lax.rsqrt(jnp.mean(centred * centred, axis=-1, keepdims=True) + 1e-05)
    unit = centred * scale
    return unit * gain + offset, unit, scale


def norm_back(grad, gain, unit, scale):
    scaled = grad * gain
    return scale * (
        scaled
        - jnp.mean(scaled, axis=-1, keepdims=True)
        - unit * jnp.mean(scaled * unit, axis=-1, keepdims=True)
    )


def shift_down(x):
    row = lax.broadcasted_iota(jnp.int32, (x.shape[0], 1), 0)
    return jnp.where(row == 0, 0.0, pltpu.roll(x, 1, 0))


def shift_up(x):
    n = x.shape[0]
    row = lax.broadcasted_iota(jnp.int32, (n, 1), 0)
    return jnp.where(row == n - 1, 0.0, pltpu.roll(x, n - 1, 0))


SPLIT = RANK_W + RANK_A


def enter_kernel(x, first, sv, hv, proj, red, exp, out, mixed_o, u_o, t_o, s_o, rkv_o, lin_o, lat_o, mix_o, a, w):
    tokens = x.shape[0]
    g = Grid(tokens, first.shape[1])
    normed, _, _ = layer_norm(x[...].astype(F32), sv[0:1], sv[1:2])
    delta = shift_down(normed) - normed
    mixes = [(normed + delta * sv[2 + c : 3 + c]).astype(BF16) for c in range(6)]
    for c in range(6):
        mix_o[c] = mixes[c]
    r = raw(mixes[0], proj[0], NN)
    k = raw(mixes[2], proj[1], NN)
    vr = raw(mixes[3], proj[2], NN)
    kind = segment(red.shape[0])
    left, right = kind[:, :SPLIT], kind[:, SPLIT:]
    ra, rb = red[:SPLIT, :], red[SPLIT:, :]
    lat = jnp.concatenate(
        [
            jnp.where(left == 0, jnp.tanh(raw(mixes[1], ra, NT)), raw(mixes[4], ra, NT)),
            jnp.where(right == 2, raw(mixes[3], rb, NT), lax.logistic(raw(mixes[5], rb, NT))),
        ],
        axis=1,
    )
    lat_o[...] = lat
    lin = [raw(jnp.where(kind == i, lat, 0.0).astype(BF16), exp[...], NN) for i in range(4)]
    for i in range(3):
        rkv_o[i] = (r, k, vr)[i]
    for i in range(4):
        lin_o[i] = lin[i]
    d, states = forward_math(
        g, r, k, vr, first[...].astype(F32), lin[0], lin[1], lin[2], hv[...], t_o, u_o, mixed_o, a, w
    )
    _, _, _, whole = tail(g, d, r, mixed_o[...])
    out[...] = whole * lin[3]
    for c in range(g.blocks):
        s_o[c] = states[c]


def channel_kernel(count, ways, where, x, cot, sv, wide, narrow, readout, *refs):
    cores, refs = refs[:count], refs[count:]
    far, refs = refs[: (count - 1) * ways], refs[(count - 1) * ways :]
    pieces, refs = refs[:count], refs[count:]
    mid_o, hid_o, dpre_o, mix_o, rows_o, buf, whole = refs
    me = where[0]
    total = raw(cores[0][...].astype(BF16), readout[...], NN)
    rows = far[0].shape[0]
    for d in range(1, count):
        for w in range(ways):
            at = pl.multiple_of(where[1 + (d - 1) * ways + w] * rows, rows)
            whole[d - 1, pl.ds(at, rows), :] = far[(d - 1) * ways + w][...].astype(BF16)
    for d in range(1, count):
        total += raw(cores[d][...].astype(BF16), whole[d - 1], NN)
    middle = x[...].astype(F32) + total
    tokens = middle.shape[0]
    share = tokens // count
    buf[...] = middle
    mid_o[...] = buf[pl.ds(pl.multiple_of(me * share, share), share), :]
    normed, unit, _ = layer_norm(middle, sv[8:9], sv[9:10])
    delta = shift_down(normed) - normed
    mix = (normed + delta * sv[10:11]).astype(BF16)
    mix_o[...] = mix
    act = jnp.maximum(raw(mix, wide[...], NN), 0.0)
    hid_o[...] = (act * act).astype(BF16)
    dpre = (raw(cot[...], narrow[...], NT) * 2.0 * act).astype(BF16)
    dpre_o[...] = dpre
    dmix = raw(dpre, wide[...], NT)
    carry = dmix * sv[10:11]
    dn = dmix - carry + shift_up(carry)
    rows_o[...] = jnp.concatenate([rowsum(dn * unit), rowsum(dn), rowsum(dmix * delta)], axis=0)
    buf[...] = dn
    for i in range(count):
        pieces[i][...] = buf[pl.ds(pl.multiple_of((me ^ i) * share, share), share), :]


def scatter_rows_kernel(count, where, x, *refs):
    for i in range(count):
        share = refs[i].shape[0]
        refs[i][...] = x[pl.ds(pl.multiple_of((where[0] ^ i) * share, share), share), :]


def gather_rows_kernel(count, where, *refs):
    out = refs[count]
    for i in range(count):
        share = refs[i].shape[0]
        out[pl.ds(pl.multiple_of((where[0] ^ i) * share, share), share), :] = refs[i][...].astype(out.dtype)


def deal_halves(value, low, keep, send, cols):
    rows = keep.shape[1]
    for p in range(value.shape[0] // (2 * rows)):
        even = value[2 * p * rows : (2 * p + 1) * rows]
        odd = value[(2 * p + 1) * rows : (2 * p + 2) * rows]
        keep[p, :, cols] = jnp.where(low == 0, even, odd)
        send[p, :, cols] = jnp.where(low == 0, odd, even)


def outer_kernel(low, mix, dpre, cot, hid, keep_a, send_a, keep_b, send_b):
    deal_halves(raw(mix[...], dpre[...], TN), low[0], keep_a, send_a, slice(None))
    deal_halves(raw(cot[...], hid[...], TN), low[0], keep_b, send_b, slice(None))


def leave_kernel(count, where, x, first, sv, hv, proj, red, exp, readout, rkv, lin, lat, mix, t, u, st, mixed, attended, *refs):
    dmid, refs = refs[:count], refs[count:]
    pieces, refs = refs[:count], refs[count:]
    first_o, head_o, exp_o, shared_o, keep_a, send_a, keep_b, send_b, dm, buf, *accs = refs
    me, low = where[0], where[1]
    tokens = x.shape[0]
    share = tokens // count
    for i in range(count):
        dm[pl.ds(pl.multiple_of((me ^ i) * share, share), share), :] = dmid[i][...]
    g = Grid(tokens, first.shape[1])
    dmb = dm[...].astype(BF16)
    d_core = raw(dmb, readout[...], NT)
    states = [st[c] for c in range(g.blocks)]
    lins = [lin[i] for i in range(4)]
    outs = backward_math(g, rkv[0], rkv[1], rkv[2], first[...].astype(F32), *lins, hv[...], t, u[...], states, mixed[...], d_core, *accs)
    first_o[...] = outs[3]
    head_o[...] = outs[8]
    d_rkv = [o.astype(BF16) for o in outs[:3]]
    d_lin = [o.astype(BF16) for o in outs[4:8]]
    lanes = red.shape[0]
    kind = segment(lanes)
    latv = lat[...]
    d_lat = jnp.zeros_like(latv)
    for i in range(4):
        d_lat = jnp.where(kind == i, raw(d_lin[i], exp[...], NT), d_lat)
    factor = jnp.where(kind == 0, 1.0 - latv * latv, jnp.where(kind == 3, latv * (1.0 - latv), 1.0))
    d_lat = d_lat * factor
    lat_stack = jnp.concatenate([jnp.where(kind == i, latv, 0.0).astype(BF16) for i in range(4)], axis=0)
    exp_o[...] = raw(lat_stack, jnp.concatenate(d_lin, axis=0), TN)
    parts = []
    for i in range(4):
        cut = slice(0, SPLIT) if i < 2 else slice(SPLIT, lanes)
        parts.append(halves(jnp.where(kind == i, d_lat, 0.0)[:, cut]))
    ra, rb = red[:SPLIT, :], red[SPLIT:, :]

    def back(i):
        w = ra if i < 2 else rb
        return raw(parts[i][0], w, NN) + raw(parts[i][1], w, NN)

    normed, unit, _ = layer_norm(x[...].astype(F32), sv[0:1], sv[1:2])
    delta = shift_down(normed) - normed
    makers = (
        lambda: raw(d_rkv[0], proj[0], NT),
        lambda: back(0),
        lambda: raw(d_rkv[1], proj[1], NT),
        lambda: raw(d_rkv[2], proj[2], NT) + back(2),
        lambda: back(1),
        lambda: back(3),
    )
    stay = carry = 0.0
    rows = []
    for c in range(6):
        grad = makers[c]()
        moved = grad * sv[2 + c : 3 + c]
        stay += grad - moved
        carry += moved
        rows.append(rowsum(grad * delta))
    dn = stay + shift_up(carry)
    shared_o[...] = jnp.concatenate([rowsum(dn * unit), rowsum(dn)] + rows, axis=0)
    buf[...] = dn
    for i in range(count):
        pieces[i][...] = buf[pl.ds(pl.multiple_of((me ^ i) * share, share), share), :]
    wide = first.shape[1]
    for i, c in enumerate((0, 2, 3)):
        deal_halves(raw(mix[c], d_rkv[i], TN), low, keep_a, send_a, slice(i * wide, (i + 1) * wide))
    deal_halves(raw(dmb, attended[...], TN), low, keep_b, send_b, slice(0, wide))

    def grown(c, i):
        return raw(mix[c], parts[i][0], TN) + raw(mix[c], parts[i][1], TN)

    deal_halves(grown(1, 0) + grown(4, 1), low, keep_b, send_b, slice(wide, wide + SPLIT))
    last = grown(3, 2) + grown(5, 3)
    last = jnp.concatenate([last, jnp.zeros((last.shape[0], keep_b.shape[2] - wide - lanes), F32)], axis=1)
    deal_halves(last, low, keep_b, send_b, slice(wide + SPLIT, keep_b.shape[2]))


VM = pl.BlockSpec(memory_space=pltpu.VMEM)
SM = pl.BlockSpec(memory_space=pltpu.SMEM)


def call(kernel, shapes, args, scratch=(), scalars=0):
    return pl.pallas_call(
        kernel,
        out_shape=tuple(jax.ShapeDtypeStruct(s, t) for s, t in shapes),
        in_specs=[SM] * scalars + [VM] * (len(args) - scalars),
        out_specs=tuple(VM for _ in shapes),
        scratch_shapes=list(scratch),
        interpret=INTERPRET,
    )(*args)


INTERPRET = False


def swap(x, axis, i, size):
    return lax.ppermute(x, axis, [(j, j ^ i) for j in range(size)])


def exchange(parts, axis):
    return [parts[0]] + [swap(parts[i], axis, i, len(parts)) for i in range(1, len(parts))]


def spread(x, axis, size):
    return [x] + [swap(x, axis, i, size) for i in range(1, size)]


def add_up(parts):
    total = parts[0]
    for p in parts[1:]:
        total = total + p
    return total


def reduce_all(x, axis, size):
    step = 1
    while step < size:
        x = x + swap(x, axis, step, size)
        step *= 2
    return x


def halve_kernel(strides, where, keep_a, got_a, keep_b, got_b, ka, sa, kb, sb):
    for n, (stride, keep, got, stay, go) in enumerate(
        ((strides[0], keep_a, got_a, ka, sa), (strides[1], keep_b, got_b, kb, sb))
    ):
        mine = where[n]
        at = 0
        for p in range(keep.shape[0]):
            if (p // stride) % 2:
                continue
            low = keep[p] + got[p]
            high = keep[p + stride] + got[p + stride]
            stay[at] = jnp.where(mine == 0, low, high)
            go[at] = jnp.where(mine == 0, high, low)
            at += 1


def halve(parts, seat, bits, left):
    keep_a, _, keep_b, _ = parts
    strides = [1 << (len(l) - 1 - l.index(bit)) for bit, l in zip(bits, left)]
    for bit, l in zip(bits, left):
        l.remove(bit)
    where = jnp.stack([(seat // bit) % 2 for bit in bits]).astype(jnp.int32)
    step = min(32, keep_a.shape[1])

    def cut(x, n):
        return pl.BlockSpec((n, step, x.shape[2]), lambda i: (0, i, 0))

    outs = (keep_a, keep_a, keep_b, keep_b)
    return pl.pallas_call(
        functools.partial(halve_kernel, strides),
        out_shape=tuple(jax.ShapeDtypeStruct((x.shape[0] // 2, *x.shape[1:]), F32) for x in outs),
        grid=(keep_a.shape[1] // step,),
        in_specs=[SM] + [cut(x, x.shape[0]) for x in parts],
        out_specs=tuple(cut(x, x.shape[0] // 2) for x in outs),
        interpret=INTERPRET,
    )(where, *parts)


def fold(quads, seat, size):
    ka, sa, kb, sb = quads
    bits = [1 << i for i in range(1, size.bit_length() - 1)]
    left = [bits[::-1], bits[::-1]]
    ga, gb = swap(sa, "dp", 1, size), swap(sb, "dp", 1, size)
    for pair in zip(bits, bits[::-1]):
        ka, sa, kb, sb = halve((ka, ga, kb, gb), seat, pair, left)
        ga, gb = swap(sa, "dp", pair[0], size), swap(sb, "dp", pair[1], size)
    return ka[0], ga[0], kb[0], gb[0]


def first_kernel(ka, ga, kb, gb, wide_o, narrow_o):
    wide_o[...] = ka[...] + ga[...]
    narrow_o[...] = (kb[...] + gb[...]).T


def second_kernel(ka, ga, kb, gb, proj_o, read_o, red_o):
    lanes = proj_o.shape[2]
    a = ka[...] + ga[...]
    b = kb[...] + gb[...]
    for i in range(3):
        proj_o[i] = a[:, i * lanes : (i + 1) * lanes]
    read_o[...] = b[:, :lanes].T
    red_o[...] = b[:, lanes : lanes + red_o.shape[1]]


def on_device(dp, tp, block_in, first_values, cotangent, shared_vectors, head_vectors, projections, reducers,
              expanders, readout, widener, narrower):
    tokens, width = block_in.shape
    lanes = first_values.shape[1]
    latents = reducers.shape[1]
    hidden = widener.shape[1]
    share = tokens // tp
    me = lax.axis_index("tensor")
    seat = lax.axis_index("dp")
    low = seat % 2
    where = jnp.stack([me, low]).astype(jnp.int32)
    bits = [1 << i for i in range(1, dp.bit_length() - 1)]

    rows = readout.shape[0] // 4
    firsts, traded, places = [], [], []
    for d in range(1, tp):
        bit = bits[d % 2]
        mine = 2 * ((seat // bit) % 2) + low
        quarter = lax.dynamic_slice_in_dim(readout, mine * rows, rows, 0).astype(F32)
        firsts.append(swap(quarter, "tensor", d, tp))
        traded.append(bit)
        places += [mine, mine ^ 2, mine ^ 1, mine ^ 3]
    spots = jnp.stack([me] + places).astype(jnp.int32)

    f, h = F32, BF16
    core_out, mixed, update, solved, states, rkv, linears, latent, mixes = call(
        enter_kernel,
        [((tokens, lanes), f), ((tokens, lanes), f), ((tokens, lanes), f), ((lanes // HEAD, tokens, tokens), f),
         ((tokens // CH, lanes, lanes), f), ((3, tokens, lanes), f), ((4, tokens, lanes), f), ((tokens, latents), f),
         ((6, tokens, width), h)],
        (block_in, first_values, shared_vectors, head_vectors, projections, reducers.T, expanders),
        scratch=[pltpu.VMEM((lanes // HEAD, tokens, tokens), F32), pltpu.VMEM((tokens, lanes), F32)],
    )
    cores = spread(core_out, "tensor", tp)
    far = []
    beside = swap(jnp.concatenate(firsts, axis=0), "dp", 1, dp)
    seconds = [swap(x, "dp", bit, dp) for x, bit in zip(firsts, traded)]
    across = swap(jnp.concatenate(seconds, axis=0), "dp", 1, dp)
    for i in range(tp - 1):
        far += [firsts[i], seconds[i], beside[i * rows : (i + 1) * rows], across[i * rows : (i + 1) * rows]]
    got = call(
        functools.partial(channel_kernel, tp, 4),
        [((share, width), f)] * tp
        + [((share, width), f), ((tokens, hidden), h), ((tokens, hidden), h), ((tokens, width), h), ((3, width), f)],
        (spots, block_in, cotangent, shared_vectors, widener, narrower, readout, *cores, *far),
        scratch=[pltpu.VMEM((tokens, width), F32), pltpu.VMEM((tp - 1, *readout.shape), BF16)], scalars=1,
    )
    pieces, (middle, hid, d_pre, mix_ffn, rows_two) = got[:tp], got[tp:]
    d_normed2 = add_up(exchange(pieces, "tensor"))
    _, unit_two, scale_two = layer_norm(middle, shared_vectors[8], shared_vectors[9])
    cot_rows = lax.dynamic_slice_in_dim(cotangent, me * share, share, 0).astype(F32)
    d_middle = cot_rows + norm_back(d_normed2, shared_vectors[8], unit_two, scale_two)
    d_mids = spread(d_middle, "tensor", tp)

    chunk = width // dp
    block = max(256, 2 * chunk)
    pairs = dp // 2
    per = block // (2 * chunk)
    half_spec = pl.BlockSpec((per, chunk, hidden), lambda i: (i, 0, 0))
    half_shape = jax.ShapeDtypeStruct((pairs, chunk, hidden), F32)
    quads = pl.pallas_call(
        outer_kernel,
        out_shape=(half_shape,) * 4,
        grid=(width // block,),
        in_specs=[SM, pl.BlockSpec((tokens, block), lambda i: (0, i)), pl.BlockSpec((tokens, hidden), lambda i: (0, 0)),
                  pl.BlockSpec((tokens, block), lambda i: (0, i)), pl.BlockSpec((tokens, hidden), lambda i: (0, 0))],
        out_specs=(half_spec,) * 4,
        name="outer", interpret=INTERPRET,
    )(where[1:], mix_ffn, d_pre, cotangent, hid)
    grad_widener, grad_narrower = call(first_kernel, [((chunk, hidden), f), ((hidden, chunk), f)],
                                       fold(quads, seat, dp))

    channel = jnp.dot(hid, narrower, preferred_element_type=F32)
    parts = call(functools.partial(scatter_rows_kernel, tp), [((share, width), f)] * tp, (where, channel), scalars=1)
    parts, _ = lax.optimization_barrier((parts, d_middle))
    block_rows = middle + add_up(exchange(parts, "tensor"))
    block_out, = call(functools.partial(gather_rows_kernel, tp), [((tokens, width), h)],
                      (where, *spread(block_rows, "tensor", tp)), scalars=1)

    attended = core_out.astype(BF16)
    wide_a = 3 * lanes
    wide_b = lanes + -(-latents // 128) * 128
    got = call(
        functools.partial(leave_kernel, tp),
        [((share, width), f)] * tp
        + [((tokens, lanes), f), ((8, lanes), f), ((latents, lanes), f), ((8, width), f)] + [((pairs, chunk, n), f) for n in (wide_a, wide_a, wide_b, wide_b)],
        (where, block_in, first_values, shared_vectors, head_vectors, projections, reducers.T, expanders, readout,
         rkv, linears, latent, mixes, solved, update, states, mixed, attended, *d_mids),
        scratch=[pltpu.VMEM((tokens, width), F32)] * 2 + [pltpu.VMEM((tokens, lanes), F32)] * 7, scalars=1,
    )
    pieces, (grad_first, local_head, local_expanders, rows_one, *quads) = got[:tp], got[tp:]
    d_normed = add_up(exchange(pieces, "tensor"))
    own = lax.dynamic_slice_in_dim(block_in, me * share, share, 0).astype(F32)
    _, unit_one, scale_one = layer_norm(own, shared_vectors[0], shared_vectors[1])
    grad_rows = d_middle + norm_back(d_normed, shared_vectors[0], unit_one, scale_one)
    grad_input, = call(functools.partial(gather_rows_kernel, tp), [((tokens, width), f)],
                       (where, *spread(grad_rows, "tensor", tp)), scalars=1)

    shared = jnp.concatenate([rows_one, rows_two], axis=0)
    small = jnp.concatenate([local_expanders, local_head, shared.reshape(-1, lanes)], axis=0)
    small = reduce_all(small, "dp", dp)
    grad_expanders = small[:latents]
    grad_head = small[latents : latents + 8]
    grad_shared = add_up(spread(small[latents + 8 :], "tensor", tp)).reshape(11, width)

    grad_projections, grad_readout, grad_reducers = call(
        second_kernel, [((3, chunk, lanes), f), ((lanes, chunk), f), ((chunk, latents), f)],
        fold(quads, seat, dp),
    )
    grad_reducers = add_up(spread(grad_reducers, "tensor", tp))
    return (block_out, grad_input, grad_first, grad_shared, grad_head, grad_projections, grad_reducers,
            grad_expanders, grad_readout, grad_widener, grad_narrower)


def solution(mesh):
    placed = (
        P("dp", None),
        P("dp", "tensor"),
        P("dp", None),
        P(),
        P(None, "tensor"),
        P(None, None, "tensor"),
        P(),
        P(None, "tensor"),
        P("tensor", None),
        P(None, "tensor"),
        P("tensor", None),
    )

    def body(*args):
        return on_device(mesh.shape["dp"], mesh.shape["tensor"], *args)

    return jax.shard_map(
        body,
        mesh=mesh,
        in_specs=placed,
        out_specs=(
            P("dp", None),
            P("dp", None),
            P("dp", "tensor"),
            P(),
            P(None, "tensor"),
            P(None, "dp", "tensor"),
            P("dp", None),
            P(None, "tensor"),
            P("tensor", "dp"),
            P("dp", "tensor"),
            P("tensor", "dp"),
        ),
        check_vma=False,
    )
```

profile of v0, /device:TPU:0, one launch (start us, length us, event | category | flops | bytes accessed | tf_op | source)
XLA Modules:
  0.0 363.9 jit_solution(8482139229018642906)
XLA Ops:
  1.7 4.1 %collective-permute-start.5 = (f32[64,1024]{1,0:T(8,128)S(1)}, f32[64,1024]{1,0:T(8,128)S(1)}, u32[]{:S(2)}, u32[]{:S(2)}) collective-permute-start(f32[64,1024]{1,0:T(8,128)S(1)} %get-tuple-element.160), channel_id=1, source_target_pairs={{0,2},{1,3},{2,0},{3,1},{4,6},{5,7},{6,4},{7,5},{8,10},{9,11},{10,... | collective-permute-start | bytes 786440 | tf_op jit(solution)/shard_map/ppermute | solution.py:535
  7.5 16.9 %collective-permute-done.5.refs_8_ = f32[64,1024]{1,0:T(8,128)S(1)} collective-permute-done((f32[64,1024]{1,0:T(8,128)S(1)}, f32[64,1024]{1,0:T(8,128)S(1)}, u32[]{:S(2)}, u32[]{:S(2)}) %collective-permute-start.5) | collective-permute-done | bytes 262176 | tf_op jit(solution)/shard_map/ppermute | solution.py:535
  24.3 1.8 collective-permute-start.8
  28.3 2.6 collective-permute-done.8.refs_9_
  30.9 3.8 %collective-permute-done.9.refs_13_ = f32[64,1024]{1,0:T(8,128)S(1)} collective-permute-done((f32[64,1024]{1,0:T(8,128)S(1)}, f32[64,1024]{1,0:T(8,128)S(1)}, u32[]{:S(2)}, u32[]{:S(2)}) %collective-permute-start.9) | collective-permute-done | bytes 262176 | tf_op jit(solution)/shard_map/ppermute | solution.py:535
  34.7 2.8 collective-permute-done.4.refs_5_
  38.6 24.2 %shard_map.194 = (f32[256,256]{1,0:T(8,128)}, f32[256,256]{1,0:T(8,128)}, f32[256,256]{1,0:T(8,128)}, f32[4,256,256]{2,1,0:T(8,128)}, f32[4,256,256]{2,1,0:T(8,1...) custom-call(bf16[256,1024]{1,0:T(8,128)(2,1)} %x.5, ...), custom_call_target="tpu_custom_call" | custom-call | tf_op jit(solution)/shard_map/pallas_call | solution.py:521
  62.8 4.6 %collective-permute-start.2 = (f32[256,256]{1,0:T(8,128)}, f32[256,256]{1,0:T(8,128)S(1)}, u32[]{:S(2)}, u32[]{:S(2)}) collective-permute-start(f32[256,256]{1,0:T(8,128)} %get-tuple-element.74.refs_0_), channel_id=1, source_target_pairs={{0,3},{1,2},{2,1},{3,0},{4,7},{5,6},{6,5},{7,4},{8,11},{9,10},{10,... | collective-permute-start | bytes 786440 | tf_op jit(solution)/shard_map/ppermute | solution.py:535
  67.4 3.6 collective-permute-start.1
  73.8 2.0 fusion.11
  75.8 15.6 %collective-permute-done.1.refs_2_ = f32[256,256]{1,0:T(8,128)S(1)} collective-permute-done((f32[256,256]{1,0:T(8,128)}, f32[256,256]{1,0:T(8,128)S(1)}, u32[]{:S(2)}, u32[]{:S(2)}) %collective-permute-start.1) | collective-permute-done | bytes 262176 | tf_op jit(solution)/shard_map/ppermute | solution.py:535
  92.2 8.1 %shard_map.195 = (f32[64,1024]{1,0:T(8,128)}, f32[64,1024]{1,0:T(8,128)}, f32[64,1024]{1,0:T(8,128)}, f32[64,1024]{1,0:T(8,128)}, f32[64,1024]{1,0:T(8,128)}, /*...) custom-call(s32[13]{0:T(128)} %stack.72.where, ...), custom_call_target="tpu_custom_call" | custom-call | tf_op jit(solution)/shard_map/pallas_call | solution.py:521
  102.4 3.3 collective-permute-start.12
  107.1 8.0 %collective-permute-done.11 = f32[64,1024]{1,0:T(8,128)S(1)} collective-permute-done((f32[64,1024]{1,0:T(8,128)}, f32[64,1024]{1,0:T(8,128)S(1)}, u32[]{:S(2)}, u32[]{:S(2)}) %collective-permute-start.11) | collective-permute-done | bytes 262176 | tf_op jit(solution)/shard_map/ppermute | solution.py:535
  115.1 9.2 %collective-permute-done.12 = f32[64,1024]{1,0:T(8,128)S(1)} collective-permute-done((f32[64,1024]{1,0:T(8,128)}, f32[64,1024]{1,0:T(8,128)S(1)}, u32[]{:S(2)}, u32[]{:S(2)}) %collective-permute-start.12) | collective-permute-done | bytes 262176 | tf_op jit(solution)/shard_map/ppermute | solution.py:535
  126.7 2.5 collective-permute-start.22
  129.2 4.3 %collective-permute-start.21 = (f32[64,1024]{1,0:T(8,128)S(1)}, f32[64,1024]{1,0:T(8,128)S(1)}, u32[]{:S(2)}, u32[]{:S(2)}) collective-permute-start(f32[64,1024]{1,0:T(8,128)S(1)} %multiply_add_fusion.refs_0_), channel_id=1, source_target_pairs={{0,2},{1,3},{2,0},{3,1},{4,6},{5,7},{6,4},{7,5},{8,10},{9,11},{10,... | collective-permute-start | bytes 786440 | tf_op jit(solution)/shard_map/ppermute | solution.py:535
  133.6 5.9 %outer.1 = (f32[4,128,1024]{2,1,0:T(8,128)}, f32[4,128,1024]{2,1,0:T(8,128)}, f32[4,128,1024]{2,1,0:T(8,128)}, f32[4,128,1024]{2,1,0:T(8,128)}) custom-call(s32[1]{0:T(128)} %bitcast.1.low, bf16[256,1024]{1,0:T(8,128)(2,1)} %get-tuple-element.121.mix, bf16[256,1024]{1,0:T(8,128)(2,1)} %get-tuple-element.122.dpre, bf16[256,1024]{1,0:T(8,128)(2,1)} %cot.3, ...), custom_call_target="tpu_custom_call" | custom-call | tf_op jit(solution)/shard_map/outer/pallas_call | solution.py:685
  141.3 10.6 %collective-permute-done.21.refs_2_ = f32[64,1024]{1,0:T(8,128)S(1)} collective-permute-done((f32[64,1024]{1,0:T(8,128)S(1)}, f32[64,1024]{1,0:T(8,128)S(1)}, u32[]{:S(2)}, u32[]{:S(2)}) %collective-permute-start.21) | collective-permute-done | bytes 262176 | tf_op jit(solution)/shard_map/ppermute | solution.py:535
  152.7 31.0 %shard_map.198 = (f32[64,1024]{1,0:T(8,128)}, f32[64,1024]{1,0:T(8,128)}, f32[64,1024]{1,0:T(8,128)}, f32[64,1024]{1,0:T(8,128)}, f32[256,256]{1,0:T(8,128)}, /*...) custom-call(s32[2]{0:T(128)} %pad_add_fusion.where, ...), custom_call_target="tpu_custom_call" | custom-call | tf_op jit(solution)/shard_map/pallas_call | solution.py:521
  185.6 2.3 shard_map.196
  188.4 8.3 %collective-permute-done.14 = f32[64,1024]{1,0:T(8,128)S(1)} collective-permute-done((f32[64,1024]{1,0:T(8,128)}, f32[64,1024]{1,0:T(8,128)S(1)}, u32[]{:S(2)}, u32[]{:S(2)}) %collective-permute-start.14) | collective-permute-done | bytes 262176 | tf_op jit(solution)/shard_map/ppermute | solution.py:535
  198.2 13.1 %collective-permute-done.15 = f32[64,1024]{1,0:T(8,128)S(1)} collective-permute-done((f32[64,1024]{1,0:T(8,128)}, f32[64,1024]{1,0:T(8,128)S(1)}, u32[]{:S(2)}, u32[]{:S(2)}) %collective-permute-start.15) | collective-permute-done | bytes 262176 | tf_op jit(solution)/shard_map/ppermute | solution.py:535
  211.3 2.4 collective-permute-start.16
  214.8 6.9 %collective-permute-done.16 = f32[64,1024]{1,0:T(8,128)S(1)} collective-permute-done((f32[64,1024]{1,0:T(8,128)}, f32[64,1024]{1,0:T(8,128)S(1)}, u32[]{:S(2)}, u32[]{:S(2)}) %collective-permute-start.16) | collective-permute-done | bytes 262176 | tf_op jit(solution)/shard_map/ppermute | solution.py:535
  221.7 3.4 collective-permute-start.23
  225.2 5.8 %collective-permute-done.23 = f32[64,1024]{1,0:T(8,128)S(1)} collective-permute-done((f32[64,1024]{1,0:T(8,128)}, f32[64,1024]{1,0:T(8,128)S(1)}, u32[]{:S(2)}, u32[]{:S(2)}) %collective-permute-start.23) | collective-permute-done | bytes 262176 | tf_op jit(solution)/shard_map/ppermute | solution.py:535
  233.2 2.4 collective-permute-start.25
  236.9 4.9 %shard_map.200 = (f32[2,128,768]{2,1,0:T(8,128)}, f32[2,128,768]{2,1,0:T(8,128)}, f32[2,128,640]{2,1,0:T(8,128)}, f32[2,128,640]{2,1,0:T(8,128)}) custom-call(s32[2]{0:T(128)} %pad_add_fusion.2.where, f32[4,128,768]{2,1,0:T(8,128)} %get-tuple-element.106.keep_a, f32[4,128,768]{2,1,0:T(8,128)} %collective-permute-done.35.got_a, ...), custom_call_target="tpu_custom_call" | custom-call | tf_op jit(solution)/shard_map/pallas_call | solution.py:589
  241.9 11.3 %collective-permute-done.24 = f32[64,1024]{1,0:T(8,128)} collective-permute-done((f32[64,1024]{1,0:T(8,128)}, f32[64,1024]{1,0:T(8,128)}, u32[]{:S(2)}, u32[]{:S(2)}) %collective-permute-start.24) | collective-permute-done | bytes 262176 | tf_op jit(solution)/shard_map/ppermute | solution.py:535
  254.6 10.3 %collective-permute-start.18 = (f32[64,1024]{1,0:T(8,128)S(1)}, f32[64,1024]{1,0:T(8,128)S(1)}, u32[]{:S(2)}, u32[]{:S(2)}) collective-permute-start(f32[64,1024]{1,0:T(8,128)S(1)} %add_add_fusion.refs_0_), channel_id=1, source_target_pairs={{0,2},{1,3},{2,0},{3,1},{4,6},{5,7},{6,4},{7,5},{8,10},{9,11},{10,... | collective-permute-start | bytes 786440 | tf_op jit(solution)/shard_map/ppermute | solution.py:535
  265.6 1.9 fusion.9
  269.2 5.8 %shard_map.203 = (f32[2,128,1024]{2,1,0:T(8,128)}, f32[2,128,1024]{2,1,0:T(8,128)}, f32[2,128,1024]{2,1,0:T(8,128)}, f32[2,128,1024]{2,1,0:T(8,128)}) custom-call(s32[2]{0:T(128)} %pad_add_fusion.2.where, f32[4,128,1024]{2,1,0:T(8,128)} %get-tuple-element.123.keep_a, f32[4,128,1024]{2,1,0:T(8,128)} %collective-permute-done.44.got_a, ...), custom_call_target="tpu_custom_call" | custom-call | tf_op jit(solution)/shard_map/pallas_call | solution.py:589
  276.5 4.2 %collective-permute-done.18.refs_2_ = f32[64,1024]{1,0:T(8,128)S(1)} collective-permute-done((f32[64,1024]{1,0:T(8,128)S(1)}, f32[64,1024]{1,0:T(8,128)S(1)}, u32[]{:S(2)}, u32[]{:S(2)}) %collective-permute-start.18) | collective-permute-done | bytes 262176 | tf_op jit(solution)/shard_map/ppermute | solution.py:535
  285.3 8.0 %collective-permute-done.30 = f32[340,256]{1,0:T(8,128)S(1)} collective-permute-done((f32[340,256]{1,0:T(8,128)S(1)}, f32[340,256]{1,0:T(8,128)S(1)}, u32[]{:S(2)}, u32[]{:S(2)}) %collective-permute-start.30) | collective-permute-done | bytes 348192 | tf_op jit(solution)/shard_map/ppermute | solution.py:535
  293.2 2.4 collective-permute-start.28
  298.8 3.9 %shard_map.201 = (f32[1,128,768]{2,1,0:T(8,128)}, f32[1,128,768]{2,1,0:T(8,128)}, f32[1,128,640]{2,1,0:T(8,128)}, f32[1,128,640]{2,1,0:T(8,128)}) custom-call(s32[2]{0:T(128)} %pad_add_fusion.1.where, f32[2,128,768]{2,1,0:T(8,128)} %get-tuple-element.110.keep_a, f32[2,128,768]{2,1,0:T(8,128)} %collective-permute-done.37.got_a, ...), custom_call_target="tpu_custom_call" | custom-call | tf_op jit(solution)/shard_map/pallas_call | solution.py:589
  303.8 11.6 %collective-permute-done.27.refs_2_ = f32[64,1024]{1,0:T(8,128)} collective-permute-done((f32[64,1024]{1,0:T(8,128)S(1)}, f32[64,1024]{1,0:T(8,128)}, u32[]{:S(2)}, u32[]{:S(2)}) %collective-permute-start.27) | collective-permute-done | bytes 262176 | tf_op jit(solution)/shard_map/ppermute | solution.py:535
  318.2 4.8 %collective-permute-done.26.refs_1_ = f32[64,1024]{1,0:T(8,128)S(1)} collective-permute-done((f32[64,1024]{1,0:T(8,128)S(1)}, f32[64,1024]{1,0:T(8,128)S(1)}, u32[]{:S(2)}, u32[]{:S(2)}) %collective-permute-start.26) | collective-permute-done | bytes 262176 | tf_op jit(solution)/shard_map/ppermute | solution.py:535
  323.9 1.8 collective-permute-start.34
  326.7 4.2 %shard_map.204 = (f32[1,128,1024]{2,1,0:T(8,128)}, f32[1,128,1024]{2,1,0:T(8,128)}, f32[1,128,1024]{2,1,0:T(8,128)}, f32[1,128,1024]{2,1,0:T(8,128)}) custom-call(s32[2]{0:T(128)} %pad_add_fusion.1.where, f32[2,128,1024]{2,1,0:T(8,128)} %get-tuple-element.127.keep_a, f32[2,128,1024]{2,1,0:T(8,128)} %copy-done.7, f32[2,128,1024]{2,1,0:T(8,128)} %get-tuple-element.129.keep_b, ...), custom_call_target="tpu_custom_call" | custom-call | tf_op jit(solution)/shard_map/pallas_call | solution.py:589
  333.9 2.0 shard_map.197
  336.0 2.2 shard_map.199
  339.6 2.2 shard_map.202
  341.8 2.0 collective-permute-start.43
  346.8 4.7 %collective-permute-done.43 = f32[128,288]{1,0:T(8,128)S(1)} collective-permute-done((f32[128,288]{1,0:T(8,128)}, f32[128,288]{1,0:T(8,128)S(1)}, u32[]{:S(2)}, u32[]{:S(2)}) %collective-permute-start.43) | collective-permute-done | bytes 147488 | tf_op jit(solution)/shard_map/ppermute | solution.py:535
  351.5 6.9 %collective-permute-done.42 = f32[128,288]{1,0:T(8,128)S(1)} collective-permute-done((f32[128,288]{1,0:T(8,128)}, f32[128,288]{1,0:T(8,128)S(1)}, u32[]{:S(2)}, u32[]{:S(2)}) %collective-permute-start.42) | collective-permute-done | bytes 147488 | tf_op jit(solution)/shard_map/ppermute | solution.py:535
  361.2 2.7 shard_map.205
  (186 shorter events, 55.3 us)
Async XLA Ops:
  1.7 22.6 %collective-permute-start.5 = (f32[64,1024]{1,0:T(8,128)S(1)}, f32[64,1024]{1,0:T(8,128)S(1)}, u32[]{:S(2)}, u32[]{:S(2)}) collective-permute-start(f32[64,1024]{1,0:T(8,128)S(1)} %get-tuple-element.160), channel_id=1, source_target_pairs={{0,2},{1,3},{2,0},{3,1},{4,6},{5,7},{6,4},{7,5},{8,10},{9,11},{10,... | collective-permute-start | bytes 786440 | tf_op jit(solution)/shard_map/ppermute | solution.py:535
  5.9 20.2 %collective-permute-start.6 = (f32[64,1024]{1,0:T(8,128)S(1)}, f32[64,1024]{1,0:T(8,128)S(1)}, u32[]{:S(2)}, u32[]{:S(2)}) collective-permute-start(f32[64,1024]{1,0:T(8,128)S(1)} %get-tuple-element.161), channel_id=1, source_target_pairs={{0,3},{1,2},{2,1},{3,0},{4,7},{5,6},{6,5},{7,4},{8,11},{9,10},{10,... | collective-permute-start | bytes 786440 | tf_op jit(solution)/shard_map/ppermute | solution.py:535
  7.2 20.4 %collective-permute-start.3 = (f32[64,1024]{1,0:T(8,128)S(1)}, f32[64,1024]{1,0:T(8,128)S(1)}, u32[]{:S(2)}, u32[]{:S(2)}) collective-permute-start(f32[64,1024]{1,0:T(8,128)S(1)} %get-tuple-element.161), channel_id=1, source_target_pairs={{0,1},{1,0},{2,3},{3,2},{4,5},{5,4},{6,7},{7,6},{8,9},{9,8},{10,11... | collective-permute-start | bytes 786440 | tf_op jit(solution)/shard_map/ppermute | solution.py:535
  26.1 8.6 %collective-permute-start.9 = (f32[64,1024]{1,0:T(8,128)S(1)}, f32[64,1024]{1,0:T(8,128)S(1)}, u32[]{:S(2)}, u32[]{:S(2)}) collective-permute-start(f32[64,1024]{1,0:T(8,128)S(1)} %collective-permute-done.6.refs_12_), channel_id=1, source_target_pairs={{0,16},{4,20},{8,24},{12,28},{16,0},{20,4},{24,8},{28,12},{1,17},{... | collective-permute-start | bytes 786440 | tf_op jit(solution)/shard_map/ppermute | solution.py:535
  27.6 9.9 %collective-permute-start.4 = (f32[64,1024]{1,0:T(8,128)S(1)}, f32[64,1024]{1,0:T(8,128)S(1)}, u32[]{:S(2)}, u32[]{:S(2)}) collective-permute-start(f32[64,1024]{1,0:T(8,128)S(1)} %collective-permute-done.3.refs_4_), channel_id=1, source_target_pairs={{0,16},{4,20},{8,24},{12,28},{16,0},{20,4},{24,8},{28,12},{1,17},{... | collective-permute-start | bytes 786440 | tf_op jit(solution)/shard_map/ppermute | solution.py:535
  28.2 44.6 %collective-permute-start.7 = (f32[192,1024]{1,0:T(8,128)S(1)}, f32[192,1024]{1,0:T(8,128)S(1)}, u32[]{:S(2)}, u32[]{:S(2)}) collective-permute-start(f32[192,1024]{1,0:T(8,128)S(1)} %pad_maximum_fusion), channel_id=1, source_target_pairs={{0,4},{4,0},{8,12},{12,8},{16,20},{20,16},{24,28},{28,24},{1,5},{5... | collective-permute-start | bytes 2359304 | tf_op jit(solution)/shard_map/ppermute | solution.py:535
  38.6 35.2 %collective-permute-start.10 = (f32[192,1024]{1,0:T(8,128)}, f32[192,1024]{1,0:T(8,128)}, u32[]{:S(2)}, u32[]{:S(2)}) collective-permute-start(f32[192,1024]{1,0:T(8,128)} %pad_maximum_fusion.1), channel_id=1, source_target_pairs={{0,4},{4,0},{8,12},{12,8},{16,20},{20,16},{24,28},{28,24},{1,5},{5... | collective-permute-start | bytes 2359304 | tf_op jit(solution)/shard_map/ppermute | solution.py:535
  62.8 13.0 %collective-permute-start.2 = (f32[256,256]{1,0:T(8,128)}, f32[256,256]{1,0:T(8,128)S(1)}, u32[]{:S(2)}, u32[]{:S(2)}) collective-permute-start(f32[256,256]{1,0:T(8,128)} %get-tuple-element.74.refs_0_), channel_id=1, source_target_pairs={{0,3},{1,2},{2,1},{3,0},{4,7},{5,6},{6,5},{7,4},{8,11},{9,10},{10,... | collective-permute-start | bytes 786440 | tf_op jit(solution)/shard_map/ppermute | solution.py:535
  67.4 24.0 %collective-permute-start.1 = (f32[256,256]{1,0:T(8,128)}, f32[256,256]{1,0:T(8,128)S(1)}, u32[]{:S(2)}, u32[]{:S(2)}) collective-permute-start(f32[256,256]{1,0:T(8,128)} %get-tuple-element.74.refs_0_), channel_id=1, source_target_pairs={{0,2},{1,3},{2,0},{3,1},{4,6},{5,7},{6,4},{7,5},{8,10},{9,11},{10,... | collective-permute-start | bytes 786440 | tf_op jit(solution)/shard_map/ppermute | solution.py:535
  70.9 20.5 %collective-permute-start = (f32[256,256]{1,0:T(8,128)}, f32[256,256]{1,0:T(8,128)S(1)}, u32[]{:S(2)}, u32[]{:S(2)}) collective-permute-start(f32[256,256]{1,0:T(8,128)} %get-tuple-element.74.refs_0_), channel_id=1, source_target_pairs={{0,1},{1,0},{2,3},{3,2},{4,5},{5,4},{6,7},{7,6},{8,9},{9,8},{10,11... | collective-permute-start | bytes 786440 | tf_op jit(solution)/shard_map/ppermute | solution.py:535
  101.5 13.6 %collective-permute-start.11 = (f32[64,1024]{1,0:T(8,128)}, f32[64,1024]{1,0:T(8,128)S(1)}, u32[]{:S(2)}, u32[]{:S(2)}) collective-permute-start(f32[64,1024]{1,0:T(8,128)} %get-tuple-element.82), channel_id=1, source_target_pairs={{0,1},{1,0},{2,3},{3,2},{4,5},{5,4},{6,7},{7,6},{8,9},{9,8},{10,11... | collective-permute-start | bytes 786440 | tf_op jit(solution)/shard_map/ppermute | solution.py:535
  102.4 21.9 %collective-permute-start.12 = (f32[64,1024]{1,0:T(8,128)}, f32[64,1024]{1,0:T(8,128)S(1)}, u32[]{:S(2)}, u32[]{:S(2)}) collective-permute-start(f32[64,1024]{1,0:T(8,128)} %get-tuple-element.83), channel_id=1, source_target_pairs={{0,2},{1,3},{2,0},{3,1},{4,6},{5,7},{6,4},{7,5},{8,10},{9,11},{10,... | collective-permute-start | bytes 786440 | tf_op jit(solution)/shard_map/ppermute | solution.py:535
  105.7 18.6 %collective-permute-start.13 = (f32[64,1024]{1,0:T(8,128)}, f32[64,1024]{1,0:T(8,128)S(1)}, u32[]{:S(2)}, u32[]{:S(2)}) collective-permute-start(f32[64,1024]{1,0:T(8,128)} %get-tuple-element.84), channel_id=1, source_target_pairs={{0,3},{1,2},{2,1},{3,0},{4,7},{5,6},{6,5},{7,4},{8,11},{9,10},{10,... | collective-permute-start | bytes 786440 | tf_op jit(solution)/shard_map/ppermute | solution.py:535
  126.7 14.6 %collective-permute-start.22 = (f32[64,1024]{1,0:T(8,128)S(1)}, f32[64,1024]{1,0:T(8,128)S(1)}, u32[]{:S(2)}, u32[]{:S(2)}) collective-permute-start(f32[64,1024]{1,0:T(8,128)S(1)} %multiply_add_fusion.refs_0_), channel_id=1, source_target_pairs={{0,3},{1,2},{2,1},{3,0},{4,7},{5,6},{6,5},{7,4},{8,11},{9,10},{10,... | collective-permute-start | bytes 786440 | tf_op jit(solution)/shard_map/ppermute | solution.py:535
  129.2 22.7 %collective-permute-start.21 = (f32[64,1024]{1,0:T(8,128)S(1)}, f32[64,1024]{1,0:T(8,128)S(1)}, u32[]{:S(2)}, u32[]{:S(2)}) collective-permute-start(f32[64,1024]{1,0:T(8,128)S(1)} %multiply_add_fusion.refs_0_), channel_id=1, source_target_pairs={{0,2},{1,3},{2,0},{3,1},{4,6},{5,7},{6,4},{7,5},{8,10},{9,11},{10,... | collective-permute-start | bytes 786440 | tf_op jit(solution)/shard_map/ppermute | solution.py:535
  133.5 18.4 %collective-permute-start.20 = (f32[64,1024]{1,0:T(8,128)S(1)}, f32[64,1024]{1,0:T(8,128)S(1)}, u32[]{:S(2)}, u32[]{:S(2)}) collective-permute-start(f32[64,1024]{1,0:T(8,128)S(1)} %multiply_add_fusion.refs_0_), channel_id=1, source_target_pairs={{0,1},{1,0},{2,3},{3,2},{4,5},{5,4},{6,7},{7,6},{8,9},{9,8},{10,11... | collective-permute-start | bytes 786440 | tf_op jit(solution)/shard_map/ppermute | solution.py:535
  139.5 125.5 %collective-permute-start.44 = (f32[4,128,1024]{2,1,0:T(8,128)}, f32[4,128,1024]{2,1,0:T(8,128)}, u32[]{:S(2)}, u32[]{:S(2)}) collective-permute-start(f32[4,128,1024]{2,1,0:T(8,128)} %get-tuple-element.124), channel_id=1, source_target_pairs={{0,4},{4,0},{8,12},{12,8},{16,20},{20,16},{24,28},{28,24},{1,5},{5... | collective-permute-start | bytes 6291464 | tf_op jit(solution)/shard_map/ppermute | solution.py:535
  140.8 126.7 %collective-permute-start.45 = (f32[4,128,1024]{2,1,0:T(8,128)}, f32[4,128,1024]{2,1,0:T(8,128)}, u32[]{:S(2)}, u32[]{:S(2)}) collective-permute-start(f32[4,128,1024]{2,1,0:T(8,128)} %get-tuple-element.126), channel_id=1, source_target_pairs={{0,4},{4,0},{8,12},{12,8},{16,20},{20,16},{24,28},{28,24},{1,5},{5... | collective-permute-start | bytes 6291464 | tf_op jit(solution)/shard_map/ppermute | solution.py:535
  183.8 49.4 %collective-permute-start.35 = (f32[4,128,768]{2,1,0:T(8,128)}, f32[4,128,768]{2,1,0:T(8,128)}, u32[]{:S(2)}, u32[]{:S(2)}) collective-permute-start(f32[4,128,768]{2,1,0:T(8,128)} %get-tuple-element.107), channel_id=1, source_target_pairs={{0,4},{4,0},{8,12},{12,8},{16,20},{20,16},{24,28},{28,24},{1,5},{5... | collective-permute-start | bytes 4718600 | tf_op jit(solution)/shard_map/ppermute | solution.py:535
  187.8 8.9 %collective-permute-start.14 = (f32[64,1024]{1,0:T(8,128)}, f32[64,1024]{1,0:T(8,128)S(1)}, u32[]{:S(2)}, u32[]{:S(2)}) collective-permute-start(f32[64,1024]{1,0:T(8,128)} %get-tuple-element.86), channel_id=1, source_target_pairs={{0,1},{1,0},{2,3},{3,2},{4,5},{5,4},{6,7},{7,6},{8,9},{9,8},{10,11... | collective-permute-start | bytes 786440 | tf_op jit(solution)/shard_map/ppermute | solution.py:535
  187.8 43.7 %collective-permute-start.36 = (f32[4,128,640]{2,1,0:T(8,128)}, f32[4,128,640]{2,1,0:T(8,128)S(1)}, u32[]{:S(2)}, u32[]{:S(2)}) collective-permute-start(f32[4,128,640]{2,1,0:T(8,128)} %get-tuple-element.109), channel_id=1, source_target_pairs={{0,4},{4,0},{8,12},{12,8},{16,20},{20,16},{24,28},{28,24},{1,5},{5... | collective-permute-start | bytes 3932168 | tf_op jit(solution)/shard_map/ppermute | solution.py:535
  196.7 14.6 %collective-permute-start.15 = (f32[64,1024]{1,0:T(8,128)}, f32[64,1024]{1,0:T(8,128)S(1)}, u32[]{:S(2)}, u32[]{:S(2)}) collective-permute-start(f32[64,1024]{1,0:T(8,128)} %get-tuple-element.87), channel_id=1, source_target_pairs={{0,2},{1,3},{2,0},{3,1},{4,6},{5,7},{6,4},{7,5},{8,10},{9,11},{10,... | collective-permute-start | bytes 786440 | tf_op jit(solution)/shard_map/ppermute | solution.py:535
  211.3 10.3 %collective-permute-start.16 = (f32[64,1024]{1,0:T(8,128)}, f32[64,1024]{1,0:T(8,128)S(1)}, u32[]{:S(2)}, u32[]{:S(2)}) collective-permute-start(f32[64,1024]{1,0:T(8,128)} %get-tuple-element.88), channel_id=1, source_target_pairs={{0,3},{1,2},{2,1},{3,0},{4,7},{5,6},{6,5},{7,4},{8,11},{9,10},{10,... | collective-permute-start | bytes 786440 | tf_op jit(solution)/shard_map/ppermute | solution.py:535
  221.7 9.3 %collective-permute-start.23 = (f32[64,1024]{1,0:T(8,128)}, f32[64,1024]{1,0:T(8,128)S(1)}, u32[]{:S(2)}, u32[]{:S(2)}) collective-permute-start(f32[64,1024]{1,0:T(8,128)} %get-tuple-element.98), channel_id=1, source_target_pairs={{0,1},{1,0},{2,3},{3,2},{4,5},{5,4},{6,7},{7,6},{8,9},{9,8},{10,11... | collective-permute-start | bytes 786440 | tf_op jit(solution)/shard_map/ppermute | solution.py:535
  230.9 33.9 %collective-permute-start.29 = (f32[340,256]{1,0:T(8,128)S(1)}, f32[340,256]{1,0:T(8,128)S(1)}, u32[]{:S(2)}, u32[]{:S(2)}) collective-permute-start(f32[340,256]{1,0:T(8,128)S(1)} %constant_dynamic-update-slice_fusion), channel_id=1, source_target_pairs={{0,4},{4,0},{8,12},{12,8},{16,20},{20,16},{24,28},{28,24},{1,5},{5... | collective-permute-start | bytes 1044488 | tf_op jit(solution)/shard_map/ppermute | solution.py:535
  231.5 21.6 %collective-permute-start.24 = (f32[64,1024]{1,0:T(8,128)}, f32[64,1024]{1,0:T(8,128)}, u32[]{:S(2)}, u32[]{:S(2)}) collective-permute-start(f32[64,1024]{1,0:T(8,128)} %get-tuple-element.99), channel_id=1, source_target_pairs={{0,2},{1,3},{2,0},{3,1},{4,6},{5,7},{6,4},{7,5},{8,10},{9,11},{10,... | collective-permute-start | bytes 786440 | tf_op jit(solution)/shard_map/ppermute | solution.py:535
  233.2 21.3 %collective-permute-start.25 = (f32[64,1024]{1,0:T(8,128)}, f32[64,1024]{1,0:T(8,128)}, u32[]{:S(2)}, u32[]{:S(2)}) collective-permute-start(f32[64,1024]{1,0:T(8,128)} %get-tuple-element.100), channel_id=1, source_target_pairs={{0,3},{1,2},{2,1},{3,0},{4,7},{5,6},{6,5},{7,4},{8,11},{9,10},{10,... | collective-permute-start | bytes 786440 | tf_op jit(solution)/shard_map/ppermute | solution.py:535
  253.2 21.8 %collective-permute-start.19 = (f32[64,1024]{1,0:T(8,128)S(1)}, f32[64,1024]{1,0:T(8,128)S(1)}, u32[]{:S(2)}, u32[]{:S(2)}) collective-permute-start(f32[64,1024]{1,0:T(8,128)S(1)} %add_add_fusion.refs_0_), channel_id=1, source_target_pairs={{0,3},{1,2},{2,1},{3,0},{4,7},{5,6},{6,5},{7,4},{8,11},{9,10},{10,... | collective-permute-start | bytes 786440 | tf_op jit(solution)/shard_map/ppermute | solution.py:535
  254.6 26.1 %collective-permute-start.18 = (f32[64,1024]{1,0:T(8,128)S(1)}, f32[64,1024]{1,0:T(8,128)S(1)}, u32[]{:S(2)}, u32[]{:S(2)}) collective-permute-start(f32[64,1024]{1,0:T(8,128)S(1)} %add_add_fusion.refs_0_), channel_id=1, source_target_pairs={{0,2},{1,3},{2,0},{3,1},{4,6},{5,7},{6,4},{7,5},{8,10},{9,11},{10,... | collective-permute-start | bytes 786440 | tf_op jit(solution)/shard_map/ppermute | solution.py:535
  264.9 17.1 %collective-permute-start.17 = (f32[64,1024]{1,0:T(8,128)S(1)}, f32[64,1024]{1,0:T(8,128)S(1)}, u32[]{:S(2)}, u32[]{:S(2)}) collective-permute-start(f32[64,1024]{1,0:T(8,128)S(1)} %add_add_fusion.refs_0_), channel_id=1, source_target_pairs={{0,1},{1,0},{2,3},{3,2},{4,5},{5,4},{6,7},{7,6},{8,9},{9,8},{10,11... | collective-permute-start | bytes 786440 | tf_op jit(solution)/shard_map/ppermute | solution.py:535
  265.0 32.2 %collective-permute-start.37 = (f32[2,128,768]{2,1,0:T(8,128)}, f32[2,128,768]{2,1,0:T(8,128)}, u32[]{:S(2)}, u32[]{:S(2)}) collective-permute-start(f32[2,128,768]{2,1,0:T(8,128)} %get-tuple-element.111), channel_id=1, source_target_pairs={{0,8},{4,12},{8,0},{12,4},{16,24},{20,28},{24,16},{28,20},{1,9},{5... | collective-permute-start | bytes 2359304 | tf_op jit(solution)/shard_map/ppermute | solution.py:535
  267.5 28.1 %collective-permute-start.38 = (f32[2,128,640]{2,1,0:T(8,128)}, f32[2,128,640]{2,1,0:T(8,128)}, u32[]{:S(2)}, u32[]{:S(2)}) collective-permute-start(f32[2,128,640]{2,1,0:T(8,128)} %get-tuple-element.113), channel_id=1, source_target_pairs={{0,16},{4,20},{8,24},{12,28},{16,0},{20,4},{24,8},{28,12},{1,17},{... | collective-permute-start | bytes 1966088 | tf_op jit(solution)/shard_map/ppermute | solution.py:535
  275.0 18.3 %collective-permute-start.30 = (f32[340,256]{1,0:T(8,128)S(1)}, f32[340,256]{1,0:T(8,128)S(1)}, u32[]{:S(2)}, u32[]{:S(2)}) collective-permute-start(f32[340,256]{1,0:T(8,128)S(1)} %add.140), channel_id=1, source_target_pairs={{0,8},{4,12},{8,0},{12,4},{16,24},{20,28},{24,16},{28,20},{1,9},{5... | collective-permute-start | bytes 1044488 | tf_op jit(solution)/shard_map/ppermute | solution.py:535
  281.4 42.5 %collective-permute-start.46 = (f32[2,128,1024]{2,1,0:T(8,128)}, f32[2,128,1024]{2,1,0:T(8,128)S(1)}, u32[]{:S(2)}, u32[]{:S(2)}) collective-permute-start(f32[2,128,1024]{2,1,0:T(8,128)} %get-tuple-element.128), channel_id=1, source_target_pairs={{0,8},{4,12},{8,0},{12,4},{16,24},{20,28},{24,16},{28,20},{1,9},{5... | collective-permute-start | bytes 3145736 | tf_op jit(solution)/shard_map/ppermute | solution.py:535
  282.6 43.1 %collective-permute-start.47 = (f32[2,128,1024]{2,1,0:T(8,128)}, f32[2,128,1024]{2,1,0:T(8,128)S(1)}, u32[]{:S(2)}, u32[]{:S(2)}) collective-permute-start(f32[2,128,1024]{2,1,0:T(8,128)} %get-tuple-element.130), channel_id=1, source_target_pairs={{0,16},{4,20},{8,24},{12,28},{16,0},{20,4},{24,8},{28,12},{1,17},{... | collective-permute-start | bytes 3145736 | tf_op jit(solution)/shard_map/ppermute | solution.py:535
  293.2 9.5 %collective-permute-start.28 = (f32[64,1024]{1,0:T(8,128)S(1)}, f32[64,1024]{1,0:T(8,128)S(1)}, u32[]{:S(2)}, u32[]{:S(2)}) collective-permute-start(f32[64,1024]{1,0:T(8,128)S(1)} %fusion.7.refs_0_), channel_id=1, source_target_pairs={{0,3},{1,2},{2,1},{3,0},{4,7},{5,6},{6,5},{7,4},{8,11},{9,10},{10,... | collective-permute-start | bytes 786440 | tf_op jit(solution)/shard_map/ppermute | solution.py:535
  295.6 20.9 %collective-permute-start.31 = (f32[340,256]{1,0:T(8,128)S(1)}, f32[340,256]{1,0:T(8,128)}, u32[]{:S(2)}, u32[]{:S(2)}) collective-permute-start(f32[340,256]{1,0:T(8,128)S(1)} %add.141), channel_id=1, source_target_pairs={{0,16},{4,20},{8,24},{12,28},{16,0},{20,4},{24,8},{28,12},{1,17},{... | collective-permute-start | bytes 1044488 | tf_op jit(solution)/shard_map/ppermute | solution.py:535
  297.3 18.2 %collective-permute-start.27 = (f32[64,1024]{1,0:T(8,128)S(1)}, f32[64,1024]{1,0:T(8,128)}, u32[]{:S(2)}, u32[]{:S(2)}) collective-permute-start(f32[64,1024]{1,0:T(8,128)S(1)} %fusion.7.refs_0_), channel_id=1, source_target_pairs={{0,2},{1,3},{2,0},{3,1},{4,6},{5,7},{6,4},{7,5},{8,10},{9,11},{10,... | collective-permute-start | bytes 786440 | tf_op jit(solution)/shard_map/ppermute | solution.py:535
  302.7 29.7 %collective-permute-start.39 = (f32[1,128,768]{2,1,0:T(8,128)}, f32[1,128,768]{2,1,0:T(8,128)S(1)}, u32[]{:S(2)}, u32[]{:S(2)}) collective-permute-start(f32[1,128,768]{2,1,0:T(8,128)} %get-tuple-element.115), channel_id=1, source_target_pairs={{0,16},{4,20},{8,24},{12,28},{16,0},{20,4},{24,8},{28,12},{1,17},{... | collective-permute-start | bytes 1179656 | tf_op jit(solution)/shard_map/ppermute | solution.py:535
  315.5 15.4 %collective-permute-start.40 = (f32[1,128,640]{2,1,0:T(8,128)}, f32[1,128,640]{2,1,0:T(8,128)}, u32[]{:S(2)}, u32[]{:S(2)}) collective-permute-start(f32[1,128,640]{2,1,0:T(8,128)} %get-tuple-element.117), channel_id=1, source_target_pairs={{0,8},{4,12},{8,0},{12,4},{16,24},{20,28},{24,16},{28,20},{1,9},{5... | collective-permute-start | bytes 983048 | tf_op jit(solution)/shard_map/ppermute | solution.py:535
  323.1 18.7 %collective-permute-start.33 = (f32[44,256]{1,0:T(8,128)}, f32[44,256]{1,0:T(8,128)S(1)}, u32[]{:S(2)}, u32[]{:S(2)}) collective-permute-start(f32[44,256]{1,0:T(8,128)} %slice.50), channel_id=1, source_target_pairs={{0,2},{1,3},{2,0},{3,1},{4,6},{5,7},{6,4},{7,5},{8,10},{9,11},{10,... | collective-permute-start | bytes 135176 | tf_op jit(solution)/shard_map/ppermute | solution.py:535
  323.9 19.9 %collective-permute-start.34 = (f32[44,256]{1,0:T(8,128)}, f32[44,256]{1,0:T(8,128)S(1)}, u32[]{:S(2)}, u32[]{:S(2)}) collective-permute-start(f32[44,256]{1,0:T(8,128)} %slice.50), channel_id=1, source_target_pairs={{0,3},{1,2},{2,1},{3,0},{4,7},{5,6},{6,5},{7,4},{8,11},{9,10},{10,... | collective-permute-start | bytes 135176 | tf_op jit(solution)/shard_map/ppermute | solution.py:535
  325.7 18.6 %collective-permute-start.32 = (f32[44,256]{1,0:T(8,128)}, f32[44,256]{1,0:T(8,128)S(1)}, u32[]{:S(2)}, u32[]{:S(2)}) collective-permute-start(f32[44,256]{1,0:T(8,128)} %slice.50), channel_id=1, source_target_pairs={{0,1},{1,0},{2,3},{3,2},{4,5},{5,4},{6,7},{7,6},{8,9},{9,8},{10,11... | collective-permute-start | bytes 135176 | tf_op jit(solution)/shard_map/ppermute | solution.py:535
  330.9 29.3 %collective-permute-start.48 = (f32[1,128,1024]{2,1,0:T(8,128)}, f32[1,128,1024]{2,1,0:T(8,128)S(1)}, u32[]{:S(2)}, u32[]{:S(2)}) collective-permute-start(f32[1,128,1024]{2,1,0:T(8,128)} %get-tuple-element.132), channel_id=1, source_target_pairs={{0,16},{4,20},{8,24},{12,28},{16,0},{20,4},{24,8},{28,12},{1,17},{... | collective-permute-start | bytes 1572872 | tf_op jit(solution)/shard_map/ppermute | solution.py:535
  332.4 27.8 %collective-permute-start.49 = (f32[1,128,1024]{2,1,0:T(8,128)}, f32[1,128,1024]{2,1,0:T(8,128)S(1)}, u32[]{:S(2)}, u32[]{:S(2)}) collective-permute-start(f32[1,128,1024]{2,1,0:T(8,128)} %get-tuple-element.134), channel_id=1, source_target_pairs={{0,8},{4,12},{8,0},{12,4},{16,24},{20,28},{24,16},{28,20},{1,9},{5... | collective-permute-start | bytes 1572872 | tf_op jit(solution)/shard_map/ppermute | solution.py:535
  341.8 9.8 %collective-permute-start.43 = (f32[128,288]{1,0:T(8,128)}, f32[128,288]{1,0:T(8,128)S(1)}, u32[]{:S(2)}, u32[]{:S(2)}) collective-permute-start(f32[128,288]{1,0:T(8,128)} %get-tuple-element.119), channel_id=1, source_target_pairs={{0,3},{1,2},{2,1},{3,0},{4,7},{5,6},{6,5},{7,4},{8,11},{9,10},{10,... | collective-permute-start | bytes 442376 | tf_op jit(solution)/shard_map/ppermute | solution.py:535
  343.8 14.6 %collective-permute-start.42 = (f32[128,288]{1,0:T(8,128)}, f32[128,288]{1,0:T(8,128)S(1)}, u32[]{:S(2)}, u32[]{:S(2)}) collective-permute-start(f32[128,288]{1,0:T(8,128)} %get-tuple-element.119), channel_id=1, source_target_pairs={{0,2},{1,3},{2,0},{3,1},{4,6},{5,7},{6,4},{7,5},{8,10},{9,11},{10,... | collective-permute-start | bytes 442376 | tf_op jit(solution)/shard_map/ppermute | solution.py:535
  344.4 14.1 %collective-permute-start.41 = (f32[128,288]{1,0:T(8,128)}, f32[128,288]{1,0:T(8,128)S(1)}, u32[]{:S(2)}, u32[]{:S(2)}) collective-permute-start(f32[128,288]{1,0:T(8,128)} %get-tuple-element.119), channel_id=1, source_target_pairs={{0,1},{1,0},{2,3},{3,2},{4,5},{5,4},{6,7},{7,6},{8,9},{9,8},{10,11... | collective-permute-start | bytes 442376 | tf_op jit(solution)/shard_map/ppermute | solution.py:535
  (41 other events, 675.0 us)
where the time goes:
time: 365 us; the launch traced here: 364 us
  waiting for transfers between devices  156 us (43%)
  Pallas kernels  99.4 us (27%)
  starting transfers between devices  77.2 us (21%)
  other arithmetic  15.9 us (4%)
  local copies, waits for them, and re-layouts  12.8 us (4%)
    ppermute x50, waiting for transfers between devices, swap(): return lax.ppermute(x, axis, [(j, j ^ i) for j in range(size)])  156 us
    ppermute x50, starting transfers between devices, swap(): return lax.ppermute(x, axis, [(j, j ^ i) for j in range(size)])  77.2 us
    pallas_call x8, Pallas kernels, call(): pl.pallas_call(kernel, out_shape=tuple((jax.ShapeDtypeStruct(s, t) for s,...  74.7 us
    pallas_call x4, Pallas kernels, halve(): pl.pallas_call(functools.partial(halve_kernel, strides), out_shape=tuple(...  18.7 us
  transfers between devices with their start and end apart: 50, of which 20 were waited for; matrix products, arithmetic and copies ran while one was open for 6% of the time, Pallas kernels for 24%

commit v1 on v0

--- a/solution.py
+++ b/solution.py
@@ -80,7 +80,7 @@
             body(h, self.mask(h))
             return carry
 
-        lax.fori_loop(0, self.heads, step, 0)
+        lax.fori_loop(0, self.heads, step, 0, unroll=2 if self.heads % 2 == 0 else 1)
 
     def seg(self, x):
         high, low = halves(x)
@@ -543,6 +543,21 @@
     return [x] + [swap(x, axis, i, size) for i in range(1, size)]
 
 
+def relay(x, axis, size):
+    if size != 4:
+        return spread(x, axis, size)
+    far = swap(x, axis, 2, size)
+    return [x, swap(x, axis, 1, size), far, swap(far, axis, 1, size)]
+
+
+def collect(parts, axis):
+    if len(parts) != 4:
+        return add_up(exchange(parts, axis))
+    joined = parts[2] + swap(parts[3], axis, 1, 4)
+    near = swap(parts[1], axis, 1, 4)
+    return parts[0] + (near + swap(joined, axis, 2, 4))
+
+
 def add_up(parts):
     total = parts[0]
     for p in parts[1:]:
@@ -699,7 +714,7 @@
     parts, _ = lax.optimization_barrier((parts, d_middle))
     block_rows = middle + add_up(exchange(parts, "tensor"))
     block_out, = call(functools.partial(gather_rows_kernel, tp), [((tokens, width), h)],
-                      (where, *spread(block_rows, "tensor", tp)), scalars=1)
+                      (where, *relay(block_rows, "tensor", tp)), scalars=1)
 
     attended = core_out.astype(BF16)
     wide_a = 3 * lanes
@@ -713,12 +728,12 @@
         scratch=[pltpu.VMEM((tokens, width), F32)] * 2 + [pltpu.VMEM((tokens, lanes), F32)] * 7, scalars=1,
     )
     pieces, (grad_first, local_head, local_expanders, rows_one, *quads) = got[:tp], got[tp:]
-    d_normed = add_up(exchange(pieces, "tensor"))
+    d_normed = collect(pieces, "tensor")
     own = lax.dynamic_slice_in_dim(block_in, me * share, share, 0).astype(F32)
     _, unit_one, scale_one = layer_norm(own, shared_vectors[0], shared_vectors[1])
     grad_rows = d_middle + norm_back(d_normed, shared_vectors[0], unit_one, scale_one)
     grad_input, = call(functools.partial(gather_rows_kernel, tp), [((tokens, width), f)],
-                       (where, *spread(grad_rows, "tensor", tp)), scalars=1)
+                       (where, *relay(grad_rows, "tensor", tp)), scalars=1)
 
     shared = jnp.concatenate([rows_one, rows_two], axis=0)
     small = jnp.concatenate([local_expanders, local_head, shared.reshape(-1, lanes)], axis=0)
@@ -731,7 +746,7 @@
         second_kernel, [((3, chunk, lanes), f), ((lanes, chunk), f), ((chunk, latents), f)],
         fold(quads, seat, dp),
     )
-    grad_reducers = add_up(spread(grad_reducers, "tensor", tp))
+    grad_reducers = add_up(relay(grad_reducers, "tensor", tp))
     return (block_out, grad_input, grad_first, grad_shared, grad_head, grad_projections, grad_reducers,
             grad_expanders, grad_readout, grad_widener, grad_narrower)
 

time: 365 us -> 316 us (0.87)
  waiting for transfers between devices: 156 us -> 115 us
  starting transfers between devices: 77.2 us -> 72.9 us
  Pallas kernels: 99.4 us -> 95.7 us
    ppermute x50, waiting for transfers between devices: 156 us -> 115 us  [swap(): return lax.ppermute(x, axis, [(j, j ^ i) for j in range(size)])]
    ppermute x50, starting transfers between devices: 77.2 us -> 72.9 us  [swap(): return lax.ppermute(x, axis, [(j, j ^ i) for j in range(size)])]
    pallas_call x8, Pallas kernels: 74.7 us -> 71 us  [call(): pl.pallas_call(kernel, out_shape=tuple((jax.ShapeDtypeStruct(s, t) for s,...]
  transfers between devices with their start and end apart: 50 -> 50, of which waited for: 20 -> 17; matrix products, arithmetic and copies ran while one was open for 6% -> 8% of each run, Pallas kernels for 24% -> 27%
where the time goes in v1:
time: 316 us; the launch traced here: 315 us
  waiting for transfers between devices  115 us (36%)
  Pallas kernels  95.7 us (30%)
  starting transfers between devices  72.9 us (23%)
  other arithmetic  18.2 us (6%)
  local copies, waits for them, and re-layouts  10.7 us (3%)
    ppermute x50, waiting for transfers between devices, swap(): return lax.ppermute(x, axis, [(j, j ^ i) for j in range(size)])  115 us
    ppermute x50, starting transfers between devices, swap(): return lax.ppermute(x, axis, [(j, j ^ i) for j in range(size)])  72.9 us
    pallas_call x8, Pallas kernels, call(): pl.pallas_call(kernel, out_shape=tuple((jax.ShapeDtypeStruct(s, t) for s,...  71 us
    pallas_call x4, Pallas kernels, halve(): pl.pallas_call(functools.partial(halve_kernel, strides), out_shape=tuple(...  18.6 us
  transfers between devices with their start and end apart: 50, of which 17 were waited for; matrix products, arithmetic and copies ran while one was open for 8% of the time, Pallas kernels for 27%

profile of v1, /device:TPU:0, one launch (start us, length us, event | category | flops | bytes accessed | tf_op | source)
XLA Modules:
  0.0 315.0 jit_solution(7768357701235792307)
XLA Ops:
  1.7 4.1 %collective-permute-start.5 = (f32[64,1024]{1,0:T(8,128)S(1)}, f32[64,1024]{1,0:T(8,128)S(1)}, u32[]{:S(2)}, u32[]{:S(2)}) collective-permute-start(f32[64,1024]{1,0:T(8,128)S(1)} %get-tuple-element.160), channel_id=1, source_target_pairs={{0,2},{1,3},{2,0},{3,1},{4,6},{5,7},{6,4},{7,5},{8,10},{9,11},{10,... | collective-permute-start | bytes 786440 | tf_op jit(solution)/shard_map/ppermute | solution.py:535
  7.5 16.9 %collective-permute-done.5.refs_8_ = f32[64,1024]{1,0:T(8,128)S(1)} collective-permute-done((f32[64,1024]{1,0:T(8,128)S(1)}, f32[64,1024]{1,0:T(8,128)S(1)}, u32[]{:S(2)}, u32[]{:S(2)}) %collective-permute-start.5) | collective-permute-done | bytes 262176 | tf_op jit(solution)/shard_map/ppermute | solution.py:535
  28.3 2.6 collective-permute-done.8.refs_9_
  30.9 3.8 %collective-permute-done.9.refs_13_ = f32[64,1024]{1,0:T(8,128)S(1)} collective-permute-done((f32[64,1024]{1,0:T(8,128)S(1)}, f32[64,1024]{1,0:T(8,128)S(1)}, u32[]{:S(2)}, u32[]{:S(2)}) %collective-permute-start.9) | collective-permute-done | bytes 262176 | tf_op jit(solution)/shard_map/ppermute | solution.py:535
  34.7 2.8 collective-permute-done.4.refs_5_
  38.5 22.0 %shard_map.194 = (f32[256,256]{1,0:T(8,128)}, f32[256,256]{1,0:T(8,128)}, f32[256,256]{1,0:T(8,128)}, f32[4,256,256]{2,1,0:T(8,128)}, f32[4,256,256]{2,1,0:T(8,1...) custom-call(bf16[256,1024]{1,0:T(8,128)(2,1)} %x.5, ...), custom_call_target="tpu_custom_call" | custom-call | tf_op jit(solution)/shard_map/pallas_call | solution.py:521
  60.7 4.6 %collective-permute-start.2 = (f32[256,256]{1,0:T(8,128)}, f32[256,256]{1,0:T(8,128)S(1)}, u32[]{:S(2)}, u32[]{:S(2)}) collective-permute-start(f32[256,256]{1,0:T(8,128)} %get-tuple-element.74.refs_0_), channel_id=1, source_target_pairs={{0,3},{1,2},{2,1},{3,0},{4,7},{5,6},{6,5},{7,4},{8,11},{9,10},{10,... | collective-permute-start | bytes 786440 | tf_op jit(solution)/shard_map/ppermute | solution.py:535
  65.2 3.6 %collective-permute-start.1 = (f32[256,256]{1,0:T(8,128)}, f32[256,256]{1,0:T(8,128)S(1)}, u32[]{:S(2)}, u32[]{:S(2)}) collective-permute-start(f32[256,256]{1,0:T(8,128)} %get-tuple-element.74.refs_0_), channel_id=1, source_target_pairs={{0,2},{1,3},{2,0},{3,1},{4,6},{5,7},{6,4},{7,5},{8,10},{9,11},{10,... | collective-permute-start | bytes 786440 | tf_op jit(solution)/shard_map/ppermute | solution.py:535
  72.3 2.0 fusion.11
  74.3 14.9 %collective-permute-done.1.refs_2_ = f32[256,256]{1,0:T(8,128)S(1)} collective-permute-done((f32[256,256]{1,0:T(8,128)}, f32[256,256]{1,0:T(8,128)S(1)}, u32[]{:S(2)}, u32[]{:S(2)}) %collective-permute-start.1) | collective-permute-done | bytes 262176 | tf_op jit(solution)/shard_map/ppermute | solution.py:535
  90.0 8.1 %shard_map.195 = (f32[64,1024]{1,0:T(8,128)}, f32[64,1024]{1,0:T(8,128)}, f32[64,1024]{1,0:T(8,128)}, f32[64,1024]{1,0:T(8,128)}, f32[64,1024]{1,0:T(8,128)}, /*...) custom-call(s32[13]{0:T(128)} %stack.72.where, ...), custom_call_target="tpu_custom_call" | custom-call | tf_op jit(solution)/shard_map/pallas_call | solution.py:521
  100.2 3.3 %collective-permute-start.12 = (f32[64,1024]{1,0:T(8,128)}, f32[64,1024]{1,0:T(8,128)}, u32[]{:S(2)}, u32[]{:S(2)}) collective-permute-start(f32[64,1024]{1,0:T(8,128)} %get-tuple-element.83), channel_id=1, source_target_pairs={{0,2},{1,3},{2,0},{3,1},{4,6},{5,7},{6,4},{7,5},{8,10},{9,11},{10,... | collective-permute-start | bytes 786440 | tf_op jit(solution)/shard_map/ppermute | solution.py:535
  105.0 6.1 %outer.1 = (f32[4,128,1024]{2,1,0:T(8,128)}, f32[4,128,1024]{2,1,0:T(8,128)}, f32[4,128,1024]{2,1,0:T(8,128)}, f32[4,128,1024]{2,1,0:T(8,128)}) custom-call(s32[1]{0:T(128)} %bitcast.1.low, bf16[256,1024]{1,0:T(8,128)(2,1)} %get-tuple-element.121.mix, bf16[256,1024]{1,0:T(8,128)(2,1)} %get-tuple-element.122.dpre, bf16[256,1024]{1,0:T(8,128)(2,1)} %cot.3, ...), custom_call_target="tpu_custom_call" | custom-call | tf_op jit(solution)/shard_map/outer/pallas_call | solution.py:700
  111.0 1.9 collective-permute-done.11
  113.0 9.3 %collective-permute-done.12 = f32[64,1024]{1,0:T(8,128)} collective-permute-done((f32[64,1024]{1,0:T(8,128)}, f32[64,1024]{1,0:T(8,128)}, u32[]{:S(2)}, u32[]{:S(2)}) %collective-permute-start.12) | collective-permute-done | bytes 262176 | tf_op jit(solution)/shard_map/ppermute | solution.py:535
  124.6 2.5 collective-permute-start.22
  127.1 4.3 %collective-permute-start.21 = (f32[64,1024]{1,0:T(8,128)S(1)}, f32[64,1024]{1,0:T(8,128)}, u32[]{:S(2)}, u32[]{:S(2)}) collective-permute-start(f32[64,1024]{1,0:T(8,128)S(1)} %multiply_add_fusion.refs_0_), channel_id=1, source_target_pairs={{0,2},{1,3},{2,0},{3,1},{4,6},{5,7},{6,4},{7,5},{8,10},{9,11},{10,... | collective-permute-start | bytes 786440 | tf_op jit(solution)/shard_map/ppermute | solution.py:535
  133.2 2.3 shard_map.196
  135.5 1.9 collective-permute-start.14
  137.4 8.6 %collective-permute-start.15 = (f32[64,1024]{1,0:T(8,128)}, f32[64,1024]{1,0:T(8,128)S(1)}, u32[]{:S(2)}, u32[]{:S(2)}) collective-permute-start(f32[64,1024]{1,0:T(8,128)} %get-tuple-element.87), channel_id=1, source_target_pairs={{0,2},{1,3},{2,0},{3,1},{4,6},{5,7},{6,4},{7,5},{8,10},{9,11},{10,... | collective-permute-start | bytes 786440 | tf_op jit(solution)/shard_map/ppermute | solution.py:535
  146.0 5.9 %collective-permute-done.21.refs_2_ = f32[64,1024]{1,0:T(8,128)} collective-permute-done((f32[64,1024]{1,0:T(8,128)S(1)}, f32[64,1024]{1,0:T(8,128)}, u32[]{:S(2)}, u32[]{:S(2)}) %collective-permute-start.21) | collective-permute-done | bytes 262176 | tf_op jit(solution)/shard_map/ppermute | solution.py:535
  152.6 29.4 %shard_map.198 = (f32[64,1024]{1,0:T(8,128)}, f32[64,1024]{1,0:T(8,128)}, f32[64,1024]{1,0:T(8,128)}, f32[64,1024]{1,0:T(8,128)}, f32[256,256]{1,0:T(8,128)}, /*...) custom-call(s32[2]{0:T(128)} %pad_add_fusion.where, ...), custom_call_target="tpu_custom_call" | custom-call | tf_op jit(solution)/shard_map/pallas_call | solution.py:521
  182.8 2.0 collective-permute-start.16
  185.8 7.6 %collective-permute-done.16 = f32[64,1024]{1,0:T(8,128)S(1)} collective-permute-done((f32[64,1024]{1,0:T(8,128)S(1)}, f32[64,1024]{1,0:T(8,128)S(1)}, u32[]{:S(2)}, u32[]{:S(2)}) %collective-permute-start.16) | collective-permute-done | bytes 262176 | tf_op jit(solution)/shard_map/ppermute | solution.py:535
  193.4 2.5 collective-permute-start.24
  197.4 4.7 %collective-permute-done.24 = f32[64,1024]{1,0:T(8,128)S(1)} collective-permute-done((f32[64,1024]{1,0:T(8,128)}, f32[64,1024]{1,0:T(8,128)S(1)}, u32[]{:S(2)}, u32[]{:S(2)}) %collective-permute-start.24) | collective-permute-done | bytes 262176 | tf_op jit(solution)/shard_map/ppermute | solution.py:535
  204.0 1.8 collective-permute-start.23
  206.4 2.0 add_add_fusion.refs_0_
  208.4 2.4 collective-permute-start.18
  210.8 4.8 %shard_map.200 = (f32[2,128,768]{2,1,0:T(8,128)}, f32[2,128,768]{2,1,0:T(8,128)}, f32[2,128,640]{2,1,0:T(8,128)}, f32[2,128,640]{2,1,0:T(8,128)}) custom-call(s32[2]{0:T(128)} %pad_add_fusion.2.where, f32[4,128,768]{2,1,0:T(8,128)} %get-tuple-element.106.keep_a, f32[4,128,768]{2,1,0:T(8,128)} %copy-done.6, f32[4,128,640]{2,1,0:T(8,128)} %get-tuple-element.108.keep_b, ...), custom_call_target="tpu_custom_call" | custom-call | tf_op jit(solution)/shard_map/pallas_call | solution.py:604
  215.6 2.4 collective-permute-done.23
  219.5 7.8 %collective-permute-done.25 = f32[64,1024]{1,0:T(8,128)} collective-permute-done((f32[64,1024]{1,0:T(8,128)S(1)}, f32[64,1024]{1,0:T(8,128)}, u32[]{:S(2)}, u32[]{:S(2)}) %collective-permute-start.25) | collective-permute-done | bytes 262176 | tf_op jit(solution)/shard_map/ppermute | solution.py:535
  227.9 1.8 fusion.9
  229.9 5.8 %shard_map.203 = (f32[2,128,1024]{2,1,0:T(8,128)}, f32[2,128,1024]{2,1,0:T(8,128)}, f32[2,128,1024]{2,1,0:T(8,128)}, f32[2,128,1024]{2,1,0:T(8,128)}) custom-call(s32[2]{0:T(128)} %pad_add_fusion.2.where, f32[4,128,1024]{2,1,0:T(8,128)} %get-tuple-element.123.keep_a, f32[4,128,1024]{2,1,0:T(8,128)} %collective-permute-done.44.got_a, ...), custom_call_target="tpu_custom_call" | custom-call | tf_op jit(solution)/shard_map/pallas_call | solution.py:604
  238.7 2.0 collective-permute-start.19
  242.3 5.8 %collective-permute-done.37.got_a = f32[2,128,768]{2,1,0:T(8,128)} collective-permute-done((f32[2,128,768]{2,1,0:T(8,128)}, f32[2,128,768]{2,1,0:T(8,128)}, u32[]{:S(2)}, u32[]{:S(2)}) %collective-permute-start.37) | collective-permute-done | bytes 786464 | tf_op jit(solution)/shard_map/ppermute | solution.py:535
  248.7 3.9 %shard_map.201 = (f32[1,128,768]{2,1,0:T(8,128)}, f32[1,128,768]{2,1,0:T(8,128)}, f32[1,128,640]{2,1,0:T(8,128)}, f32[1,128,640]{2,1,0:T(8,128)}) custom-call(s32[2]{0:T(128)} %pad_add_fusion.1.where, f32[2,128,768]{2,1,0:T(8,128)} %get-tuple-element.110.keep_a, f32[2,128,768]{2,1,0:T(8,128)} %collective-permute-done.37.got_a, ...), custom_call_target="tpu_custom_call" | custom-call | tf_op jit(solution)/shard_map/pallas_call | solution.py:604
  254.2 18.9 %collective-permute-done.30 = f32[340,256]{1,0:T(8,128)} collective-permute-done((f32[340,256]{1,0:T(8,128)S(1)}, f32[340,256]{1,0:T(8,128)}, u32[]{:S(2)}, u32[]{:S(2)}) %collective-permute-start.30) | collective-permute-done | bytes 348192 | tf_op jit(solution)/shard_map/ppermute | solution.py:535
  276.3 4.0 %collective-permute-done.40 = f32[1,128,640]{2,1,0:T(8,128)S(1)} collective-permute-done((f32[1,128,640]{2,1,0:T(8,128)}, f32[1,128,640]{2,1,0:T(8,128)S(1)}, u32[]{:S(2)}, u32[]{:S(2)}) %collective-permute-start.40) | collective-permute-done | bytes 327712 | tf_op jit(solution)/shard_map/ppermute | solution.py:535
  282.3 2.2 shard_map.202
  287.7 2.0 collective-permute-start.34
  289.7 4.2 %shard_map.204 = (f32[1,128,1024]{2,1,0:T(8,128)}, f32[1,128,1024]{2,1,0:T(8,128)}, f32[1,128,1024]{2,1,0:T(8,128)}, f32[1,128,1024]{2,1,0:T(8,128)}) custom-call(s32[2]{0:T(128)} %pad_add_fusion.1.where, f32[2,128,1024]{2,1,0:T(8,128)} %get-tuple-element.127.keep_a, f32[2,128,1024]{2,1,0:T(8,128)} %copy-done.7, f32[2,128,1024]{2,1,0:T(8,128)} %get-tuple-element.129.keep_b, ...), custom_call_target="tpu_custom_call" | custom-call | tf_op jit(solution)/shard_map/pallas_call | solution.py:604
  296.0 2.0 shard_map.197
  299.4 2.2 shard_map.199
  301.7 2.0 collective-permute-start.41
  304.4 3.0 collective-permute-done.41
  307.4 2.2 collective-permute-done.43
  312.3 2.7 shard_map.205
  (171 shorter events, 50.3 us)
Async XLA Ops:
  1.7 22.6 %collective-permute-start.5 = (f32[64,1024]{1,0:T(8,128)S(1)}, f32[64,1024]{1,0:T(8,128)S(1)}, u32[]{:S(2)}, u32[]{:S(2)}) collective-permute-start(f32[64,1024]{1,0:T(8,128)S(1)} %get-tuple-element.160), channel_id=1, source_target_pairs={{0,2},{1,3},{2,0},{3,1},{4,6},{5,7},{6,4},{7,5},{8,10},{9,11},{10,... | collective-permute-start | bytes 786440 | tf_op jit(solution)/shard_map/ppermute | solution.py:535
  5.9 20.2 %collective-permute-start.6 = (f32[64,1024]{1,0:T(8,128)S(1)}, f32[64,1024]{1,0:T(8,128)S(1)}, u32[]{:S(2)}, u32[]{:S(2)}) collective-permute-start(f32[64,1024]{1,0:T(8,128)S(1)} %get-tuple-element.161), channel_id=1, source_target_pairs={{0,3},{1,2},{2,1},{3,0},{4,7},{5,6},{6,5},{7,4},{8,11},{9,10},{10,... | collective-permute-start | bytes 786440 | tf_op jit(solution)/shard_map/ppermute | solution.py:535
  7.2 20.4 %collective-permute-start.3 = (f32[64,1024]{1,0:T(8,128)S(1)}, f32[64,1024]{1,0:T(8,128)S(1)}, u32[]{:S(2)}, u32[]{:S(2)}) collective-permute-start(f32[64,1024]{1,0:T(8,128)S(1)} %get-tuple-element.161), channel_id=1, source_target_pairs={{0,1},{1,0},{2,3},{3,2},{4,5},{5,4},{6,7},{7,6},{8,9},{9,8},{10,11... | collective-permute-start | bytes 786440 | tf_op jit(solution)/shard_map/ppermute | solution.py:535
  24.3 6.6 %collective-permute-start.8 = (f32[64,1024]{1,0:T(8,128)S(1)}, f32[64,1024]{1,0:T(8,128)S(1)}, u32[]{:S(2)}, u32[]{:S(2)}) collective-permute-start(f32[64,1024]{1,0:T(8,128)S(1)} %collective-permute-done.5.refs_8_), channel_id=1, source_target_pairs={{0,8},{4,12},{8,0},{12,4},{16,24},{20,28},{24,16},{28,20},{1,9},{5... | collective-permute-start | bytes 786440 | tf_op jit(solution)/shard_map/ppermute | solution.py:535
  26.1 8.6 %collective-permute-start.9 = (f32[64,1024]{1,0:T(8,128)S(1)}, f32[64,1024]{1,0:T(8,128)S(1)}, u32[]{:S(2)}, u32[]{:S(2)}) collective-permute-start(f32[64,1024]{1,0:T(8,128)S(1)} %collective-permute-done.6.refs_12_), channel_id=1, source_target_pairs={{0,16},{4,20},{8,24},{12,28},{16,0},{20,4},{24,8},{28,12},{1,17},{... | collective-permute-start | bytes 786440 | tf_op jit(solution)/shard_map/ppermute | solution.py:535
  27.6 9.9 %collective-permute-start.4 = (f32[64,1024]{1,0:T(8,128)S(1)}, f32[64,1024]{1,0:T(8,128)S(1)}, u32[]{:S(2)}, u32[]{:S(2)}) collective-permute-start(f32[64,1024]{1,0:T(8,128)S(1)} %collective-permute-done.3.refs_4_), channel_id=1, source_target_pairs={{0,16},{4,20},{8,24},{12,28},{16,0},{20,4},{24,8},{28,12},{1,17},{... | collective-permute-start | bytes 786440 | tf_op jit(solution)/shard_map/ppermute | solution.py:535
  28.2 43.1 %collective-permute-start.7 = (f32[192,1024]{1,0:T(8,128)S(1)}, f32[192,1024]{1,0:T(8,128)S(1)}, u32[]{:S(2)}, u32[]{:S(2)}) collective-permute-start(f32[192,1024]{1,0:T(8,128)S(1)} %pad_maximum_fusion), channel_id=1, source_target_pairs={{0,4},{4,0},{8,12},{12,8},{16,20},{20,16},{24,28},{28,24},{1,5},{5... | collective-permute-start | bytes 2359304 | tf_op jit(solution)/shard_map/ppermute | solution.py:535
  38.5 33.7 %collective-permute-start.10 = (f32[192,1024]{1,0:T(8,128)}, f32[192,1024]{1,0:T(8,128)}, u32[]{:S(2)}, u32[]{:S(2)}) collective-permute-start(f32[192,1024]{1,0:T(8,128)} %pad_maximum_fusion.1), channel_id=1, source_target_pairs={{0,4},{4,0},{8,12},{12,8},{16,20},{20,16},{24,28},{28,24},{1,5},{5... | collective-permute-start | bytes 2359304 | tf_op jit(solution)/shard_map/ppermute | solution.py:535
  60.7 13.6 %collective-permute-start.2 = (f32[256,256]{1,0:T(8,128)}, f32[256,256]{1,0:T(8,128)S(1)}, u32[]{:S(2)}, u32[]{:S(2)}) collective-permute-start(f32[256,256]{1,0:T(8,128)} %get-tuple-element.74.refs_0_), channel_id=1, source_target_pairs={{0,3},{1,2},{2,1},{3,0},{4,7},{5,6},{6,5},{7,4},{8,11},{9,10},{10,... | collective-permute-start | bytes 786440 | tf_op jit(solution)/shard_map/ppermute | solution.py:535
  65.2 24.0 %collective-permute-start.1 = (f32[256,256]{1,0:T(8,128)}, f32[256,256]{1,0:T(8,128)S(1)}, u32[]{:S(2)}, u32[]{:S(2)}) collective-permute-start(f32[256,256]{1,0:T(8,128)} %get-tuple-element.74.refs_0_), channel_id=1, source_target_pairs={{0,2},{1,3},{2,0},{3,1},{4,6},{5,7},{6,4},{7,5},{8,10},{9,11},{10,... | collective-permute-start | bytes 786440 | tf_op jit(solution)/shard_map/ppermute | solution.py:535
  68.8 20.5 %collective-permute-start = (f32[256,256]{1,0:T(8,128)}, f32[256,256]{1,0:T(8,128)S(1)}, u32[]{:S(2)}, u32[]{:S(2)}) collective-permute-start(f32[256,256]{1,0:T(8,128)} %get-tuple-element.74.refs_0_), channel_id=1, source_target_pairs={{0,1},{1,0},{2,3},{3,2},{4,5},{5,4},{6,7},{7,6},{8,9},{9,8},{10,11... | collective-permute-start | bytes 786440 | tf_op jit(solution)/shard_map/ppermute | solution.py:535
  99.3 13.7 %collective-permute-start.11 = (f32[64,1024]{1,0:T(8,128)}, f32[64,1024]{1,0:T(8,128)S(1)}, u32[]{:S(2)}, u32[]{:S(2)}) collective-permute-start(f32[64,1024]{1,0:T(8,128)} %get-tuple-element.82), channel_id=1, source_target_pairs={{0,1},{1,0},{2,3},{3,2},{4,5},{5,4},{6,7},{7,6},{8,9},{9,8},{10,11... | collective-permute-start | bytes 786440 | tf_op jit(solution)/shard_map/ppermute | solution.py:535
  100.2 22.0 %collective-permute-start.12 = (f32[64,1024]{1,0:T(8,128)}, f32[64,1024]{1,0:T(8,128)}, u32[]{:S(2)}, u32[]{:S(2)}) collective-permute-start(f32[64,1024]{1,0:T(8,128)} %get-tuple-element.83), channel_id=1, source_target_pairs={{0,2},{1,3},{2,0},{3,1},{4,6},{5,7},{6,4},{7,5},{8,10},{9,11},{10,... | collective-permute-start | bytes 786440 | tf_op jit(solution)/shard_map/ppermute | solution.py:535
  103.5 18.8 %collective-permute-start.13 = (f32[64,1024]{1,0:T(8,128)}, f32[64,1024]{1,0:T(8,128)}, u32[]{:S(2)}, u32[]{:S(2)}) collective-permute-start(f32[64,1024]{1,0:T(8,128)} %get-tuple-element.84), channel_id=1, source_target_pairs={{0,3},{1,2},{2,1},{3,0},{4,7},{5,6},{6,5},{7,4},{8,11},{9,10},{10,... | collective-permute-start | bytes 786440 | tf_op jit(solution)/shard_map/ppermute | solution.py:535
  111.0 118.7 %collective-permute-start.44 = (f32[4,128,1024]{2,1,0:T(8,128)}, f32[4,128,1024]{2,1,0:T(8,128)}, u32[]{:S(2)}, u32[]{:S(2)}) collective-permute-start(f32[4,128,1024]{2,1,0:T(8,128)} %get-tuple-element.124), channel_id=1, source_target_pairs={{0,4},{4,0},{8,12},{12,8},{16,20},{20,16},{24,28},{28,24},{1,5},{5... | collective-permute-start | bytes 6291464 | tf_op jit(solution)/shard_map/ppermute | solution.py:535
  124.6 12.8 %collective-permute-start.22 = (f32[64,1024]{1,0:T(8,128)S(1)}, f32[64,1024]{1,0:T(8,128)}, u32[]{:S(2)}, u32[]{:S(2)}) collective-permute-start(f32[64,1024]{1,0:T(8,128)S(1)} %multiply_add_fusion.refs_0_), channel_id=1, source_target_pairs={{0,3},{1,2},{2,1},{3,0},{4,7},{5,6},{6,5},{7,4},{8,11},{9,10},{10,... | collective-permute-start | bytes 786440 | tf_op jit(solution)/shard_map/ppermute | solution.py:535
  127.1 24.8 %collective-permute-start.21 = (f32[64,1024]{1,0:T(8,128)S(1)}, f32[64,1024]{1,0:T(8,128)}, u32[]{:S(2)}, u32[]{:S(2)}) collective-permute-start(f32[64,1024]{1,0:T(8,128)S(1)} %multiply_add_fusion.refs_0_), channel_id=1, source_target_pairs={{0,2},{1,3},{2,0},{3,1},{4,6},{5,7},{6,4},{7,5},{8,10},{9,11},{10,... | collective-permute-start | bytes 786440 | tf_op jit(solution)/shard_map/ppermute | solution.py:535
  131.4 21.1 %collective-permute-start.20 = (f32[64,1024]{1,0:T(8,128)S(1)}, f32[64,1024]{1,0:T(8,128)}, u32[]{:S(2)}, u32[]{:S(2)}) collective-permute-start(f32[64,1024]{1,0:T(8,128)S(1)} %multiply_add_fusion.refs_0_), channel_id=1, source_target_pairs={{0,1},{1,0},{2,3},{3,2},{4,5},{5,4},{6,7},{7,6},{8,9},{9,8},{10,11... | collective-permute-start | bytes 786440 | tf_op jit(solution)/shard_map/ppermute | solution.py:535
  135.5 47.1 %collective-permute-start.14 = (f32[64,1024]{1,0:T(8,128)}, f32[64,1024]{1,0:T(8,128)}, u32[]{:S(2)}, u32[]{:S(2)}) collective-permute-start(f32[64,1024]{1,0:T(8,128)} %get-tuple-element.86), channel_id=1, source_target_pairs={{0,1},{1,0},{2,3},{3,2},{4,5},{5,4},{6,7},{7,6},{8,9},{9,8},{10,11... | collective-permute-start | bytes 786440 | tf_op jit(solution)/shard_map/ppermute | solution.py:535
  137.4 45.4 %collective-permute-start.15 = (f32[64,1024]{1,0:T(8,128)}, f32[64,1024]{1,0:T(8,128)S(1)}, u32[]{:S(2)}, u32[]{:S(2)}) collective-permute-start(f32[64,1024]{1,0:T(8,128)} %get-tuple-element.87), channel_id=1, source_target_pairs={{0,2},{1,3},{2,0},{3,1},{4,6},{5,7},{6,4},{7,5},{8,10},{9,11},{10,... | collective-permute-start | bytes 786440 | tf_op jit(solution)/shard_map/ppermute | solution.py:535
  151.9 77.9 %collective-permute-start.45 = (f32[4,128,1024]{2,1,0:T(8,128)}, f32[4,128,1024]{2,1,0:T(8,128)}, u32[]{:S(2)}, u32[]{:S(2)}) collective-permute-start(f32[4,128,1024]{2,1,0:T(8,128)} %get-tuple-element.126), channel_id=1, source_target_pairs={{0,4},{4,0},{8,12},{12,8},{16,20},{20,16},{24,28},{28,24},{1,5},{5... | collective-permute-start | bytes 6291464 | tf_op jit(solution)/shard_map/ppermute | solution.py:535
  182.0 23.8 %collective-permute-start.36 = (f32[4,128,640]{2,1,0:T(8,128)}, f32[4,128,640]{2,1,0:T(8,128)}, u32[]{:S(2)}, u32[]{:S(2)}) collective-permute-start(f32[4,128,640]{2,1,0:T(8,128)} %get-tuple-element.109), channel_id=1, source_target_pairs={{0,4},{4,0},{8,12},{12,8},{16,20},{20,16},{24,28},{28,24},{1,5},{5... | collective-permute-start | bytes 3932168 | tf_op jit(solution)/shard_map/ppermute | solution.py:535
  182.6 25.8 %collective-permute-start.35 = (f32[4,128,768]{2,1,0:T(8,128)}, f32[4,128,768]{2,1,0:T(8,128)S(1)}, u32[]{:S(2)}, u32[]{:S(2)}) collective-permute-start(f32[4,128,768]{2,1,0:T(8,128)} %get-tuple-element.107), channel_id=1, source_target_pairs={{0,4},{4,0},{8,12},{12,8},{16,20},{20,16},{24,28},{28,24},{1,5},{5... | collective-permute-start | bytes 4718600 | tf_op jit(solution)/shard_map/ppermute | solution.py:535
  182.8 10.6 %collective-permute-start.16 = (f32[64,1024]{1,0:T(8,128)S(1)}, f32[64,1024]{1,0:T(8,128)S(1)}, u32[]{:S(2)}, u32[]{:S(2)}) collective-permute-start(f32[64,1024]{1,0:T(8,128)S(1)} %copy-done.30), channel_id=1, source_target_pairs={{0,3},{1,2},{2,1},{3,0},{4,7},{5,6},{6,5},{7,4},{8,11},{9,10},{10,... | collective-permute-start | bytes 786440 | tf_op jit(solution)/shard_map/ppermute | solution.py:535
  193.4 8.7 %collective-permute-start.24 = (f32[64,1024]{1,0:T(8,128)}, f32[64,1024]{1,0:T(8,128)S(1)}, u32[]{:S(2)}, u32[]{:S(2)}) collective-permute-start(f32[64,1024]{1,0:T(8,128)} %get-tuple-element.100), channel_id=1, source_target_pairs={{0,1},{1,0},{2,3},{3,2},{4,5},{5,4},{6,7},{7,6},{8,9},{9,8},{10,11... | collective-permute-start | bytes 786440 | tf_op jit(solution)/shard_map/ppermute | solution.py:535
  204.0 14.0 %collective-permute-start.23 = (f32[64,1024]{1,0:T(8,128)}, f32[64,1024]{1,0:T(8,128)S(1)}, u32[]{:S(2)}, u32[]{:S(2)}) collective-permute-start(f32[64,1024]{1,0:T(8,128)} %get-tuple-element.98), channel_id=1, source_target_pairs={{0,1},{1,0},{2,3},{3,2},{4,5},{5,4},{6,7},{7,6},{8,9},{9,8},{10,11... | collective-permute-start | bytes 786440 | tf_op jit(solution)/shard_map/ppermute | solution.py:535
  205.8 21.6 %collective-permute-start.25 = (f32[64,1024]{1,0:T(8,128)S(1)}, f32[64,1024]{1,0:T(8,128)}, u32[]{:S(2)}, u32[]{:S(2)}) collective-permute-start(f32[64,1024]{1,0:T(8,128)S(1)} %add.136), channel_id=1, source_target_pairs={{0,2},{1,3},{2,0},{3,1},{4,6},{5,7},{6,4},{7,5},{8,10},{9,11},{10,... | collective-permute-start | bytes 786440 | tf_op jit(solution)/shard_map/ppermute | solution.py:535
  208.4 28.7 %collective-permute-start.18 = (f32[64,1024]{1,0:T(8,128)}, f32[64,1024]{1,0:T(8,128)}, u32[]{:S(2)}, u32[]{:S(2)}) collective-permute-start(f32[64,1024]{1,0:T(8,128)} %add_add_fusion.refs_0_), channel_id=1, source_target_pairs={{0,2},{1,3},{2,0},{3,1},{4,6},{5,7},{6,4},{7,5},{8,10},{9,11},{10,... | collective-permute-start | bytes 786440 | tf_op jit(solution)/shard_map/ppermute | solution.py:535
  218.0 22.7 %collective-permute-start.38 = (f32[2,128,640]{2,1,0:T(8,128)}, f32[2,128,640]{2,1,0:T(8,128)}, u32[]{:S(2)}, u32[]{:S(2)}) collective-permute-start(f32[2,128,640]{2,1,0:T(8,128)} %get-tuple-element.113), channel_id=1, source_target_pairs={{0,16},{4,20},{8,24},{12,28},{16,0},{20,4},{24,8},{28,12},{1,17},{... | collective-permute-start | bytes 1966088 | tf_op jit(solution)/shard_map/ppermute | solution.py:535
  227.4 20.7 %collective-permute-start.37 = (f32[2,128,768]{2,1,0:T(8,128)}, f32[2,128,768]{2,1,0:T(8,128)}, u32[]{:S(2)}, u32[]{:S(2)}) collective-permute-start(f32[2,128,768]{2,1,0:T(8,128)} %get-tuple-element.111), channel_id=1, source_target_pairs={{0,8},{4,12},{8,0},{12,4},{16,24},{20,28},{24,16},{28,20},{1,9},{5... | collective-permute-start | bytes 2359304 | tf_op jit(solution)/shard_map/ppermute | solution.py:535
  229.7 8.9 %collective-permute-start.17 = (f32[64,1024]{1,0:T(8,128)}, f32[64,1024]{1,0:T(8,128)S(1)}, u32[]{:S(2)}, u32[]{:S(2)}) collective-permute-start(f32[64,1024]{1,0:T(8,128)} %add_add_fusion.refs_0_), channel_id=1, source_target_pairs={{0,1},{1,0},{2,3},{3,2},{4,5},{5,4},{6,7},{7,6},{8,9},{9,8},{10,11... | collective-permute-start | bytes 786440 | tf_op jit(solution)/shard_map/ppermute | solution.py:535
  235.6 50.4 %collective-permute-start.46 = (f32[2,128,1024]{2,1,0:T(8,128)}, f32[2,128,1024]{2,1,0:T(8,128)S(1)}, u32[]{:S(2)}, u32[]{:S(2)}) collective-permute-start(f32[2,128,1024]{2,1,0:T(8,128)} %get-tuple-element.128), channel_id=1, source_target_pairs={{0,8},{4,12},{8,0},{12,4},{16,24},{20,28},{24,16},{28,20},{1,9},{5... | collective-permute-start | bytes 3145736 | tf_op jit(solution)/shard_map/ppermute | solution.py:535
  237.1 50.6 %collective-permute-start.47 = (f32[2,128,1024]{2,1,0:T(8,128)}, f32[2,128,1024]{2,1,0:T(8,128)S(1)}, u32[]{:S(2)}, u32[]{:S(2)}) collective-permute-start(f32[2,128,1024]{2,1,0:T(8,128)} %get-tuple-element.130), channel_id=1, source_target_pairs={{0,16},{4,20},{8,24},{12,28},{16,0},{20,4},{24,8},{28,12},{1,17},{... | collective-permute-start | bytes 3145736 | tf_op jit(solution)/shard_map/ppermute | solution.py:535
  238.7 13.9 %collective-permute-start.19 = (f32[64,1024]{1,0:T(8,128)}, f32[64,1024]{1,0:T(8,128)}, u32[]{:S(2)}, u32[]{:S(2)}) collective-permute-start(f32[64,1024]{1,0:T(8,128)} %collective-permute-done.18.refs_2_), channel_id=1, source_target_pairs={{0,1},{1,0},{2,3},{3,2},{4,5},{5,4},{6,7},{7,6},{8,9},{9,8},{10,11... | collective-permute-start | bytes 786440 | tf_op jit(solution)/shard_map/ppermute | solution.py:535
  240.7 32.3 %collective-permute-start.30 = (f32[340,256]{1,0:T(8,128)S(1)}, f32[340,256]{1,0:T(8,128)}, u32[]{:S(2)}, u32[]{:S(2)}) collective-permute-start(f32[340,256]{1,0:T(8,128)S(1)} %add.140), channel_id=1, source_target_pairs={{0,8},{4,12},{8,0},{12,4},{16,24},{20,28},{24,16},{28,20},{1,9},{5... | collective-permute-start | bytes 1044488 | tf_op jit(solution)/shard_map/ppermute | solution.py:535
  248.1 26.7 %collective-permute-start.27 = (f32[64,1024]{1,0:T(8,128)S(1)}, f32[64,1024]{1,0:T(8,128)}, u32[]{:S(2)}, u32[]{:S(2)}) collective-permute-start(f32[64,1024]{1,0:T(8,128)S(1)} %fusion.7.refs_0_), channel_id=1, source_target_pairs={{0,2},{1,3},{2,0},{3,1},{4,6},{5,7},{6,4},{7,5},{8,10},{9,11},{10,... | collective-permute-start | bytes 786440 | tf_op jit(solution)/shard_map/ppermute | solution.py:535
  252.6 28.4 %collective-permute-start.39 = (f32[1,128,768]{2,1,0:T(8,128)}, f32[1,128,768]{2,1,0:T(8,128)}, u32[]{:S(2)}, u32[]{:S(2)}) collective-permute-start(f32[1,128,768]{2,1,0:T(8,128)} %get-tuple-element.115), channel_id=1, source_target_pairs={{0,16},{4,20},{8,24},{12,28},{16,0},{20,4},{24,8},{28,12},{1,17},{... | collective-permute-start | bytes 1179656 | tf_op jit(solution)/shard_map/ppermute | solution.py:535
  273.0 7.3 %collective-permute-start.40 = (f32[1,128,640]{2,1,0:T(8,128)}, f32[1,128,640]{2,1,0:T(8,128)S(1)}, u32[]{:S(2)}, u32[]{:S(2)}) collective-permute-start(f32[1,128,640]{2,1,0:T(8,128)} %get-tuple-element.117), channel_id=1, source_target_pairs={{0,8},{4,12},{8,0},{12,4},{16,24},{20,28},{24,16},{28,20},{1,9},{5... | collective-permute-start | bytes 983048 | tf_op jit(solution)/shard_map/ppermute | solution.py:535
  274.8 9.8 %collective-permute-start.31 = (f32[340,256]{1,0:T(8,128)S(1)}, f32[340,256]{1,0:T(8,128)S(1)}, u32[]{:S(2)}, u32[]{:S(2)}) collective-permute-start(f32[340,256]{1,0:T(8,128)S(1)} %add.141), channel_id=1, source_target_pairs={{0,16},{4,20},{8,24},{12,28},{16,0},{20,4},{24,8},{28,12},{1,17},{... | collective-permute-start | bytes 1044488 | tf_op jit(solution)/shard_map/ppermute | solution.py:535
  280.3 13.5 %collective-permute-start.26 = (f32[64,1024]{1,0:T(8,128)S(1)}, f32[64,1024]{1,0:T(8,128)}, u32[]{:S(2)}, u32[]{:S(2)}) collective-permute-start(f32[64,1024]{1,0:T(8,128)S(1)} %fusion.7.refs_0_), channel_id=1, source_target_pairs={{0,1},{1,0},{2,3},{3,2},{4,5},{5,4},{6,7},{7,6},{8,9},{9,8},{10,11... | collective-permute-start | bytes 786440 | tf_op jit(solution)/shard_map/ppermute | solution.py:535
  281.0 12.9 %collective-permute-start.28 = (f32[64,1024]{1,0:T(8,128)}, f32[64,1024]{1,0:T(8,128)}, u32[]{:S(2)}, u32[]{:S(2)}) collective-permute-start(f32[64,1024]{1,0:T(8,128)} %collective-permute-done.27.refs_2_), channel_id=1, source_target_pairs={{0,1},{1,0},{2,3},{3,2},{4,5},{5,4},{6,7},{7,6},{8,9},{9,8},{10,11... | collective-permute-start | bytes 786440 | tf_op jit(solution)/shard_map/ppermute | solution.py:535
  284.5 19.1 %collective-permute-start.42 = (f32[128,288]{1,0:T(8,128)}, f32[128,288]{1,0:T(8,128)}, u32[]{:S(2)}, u32[]{:S(2)}) collective-permute-start(f32[128,288]{1,0:T(8,128)} %get-tuple-element.119), channel_id=1, source_target_pairs={{0,2},{1,3},{2,0},{3,1},{4,6},{5,7},{6,4},{7,5},{8,10},{9,11},{10,... | collective-permute-start | bytes 442376 | tf_op jit(solution)/shard_map/ppermute | solution.py:535
  286.0 9.5 %collective-permute-start.33 = (f32[44,256]{1,0:T(8,128)S(1)}, f32[44,256]{1,0:T(8,128)S(1)}, u32[]{:S(2)}, u32[]{:S(2)}) collective-permute-start(f32[44,256]{1,0:T(8,128)S(1)} %slice.50), channel_id=1, source_target_pairs={{0,2},{1,3},{2,0},{3,1},{4,6},{5,7},{6,4},{7,5},{8,10},{9,11},{10,... | collective-permute-start | bytes 135176 | tf_op jit(solution)/shard_map/ppermute | solution.py:535
  287.7 14.0 %collective-permute-start.34 = (f32[44,256]{1,0:T(8,128)S(1)}, f32[44,256]{1,0:T(8,128)S(1)}, u32[]{:S(2)}, u32[]{:S(2)}) collective-permute-start(f32[44,256]{1,0:T(8,128)S(1)} %slice.50), channel_id=1, source_target_pairs={{0,3},{1,2},{2,1},{3,0},{4,7},{5,6},{6,5},{7,4},{8,11},{9,10},{10,... | collective-permute-start | bytes 135176 | tf_op jit(solution)/shard_map/ppermute | solution.py:535
  293.8 9.9 %collective-permute-start.32 = (f32[44,256]{1,0:T(8,128)S(1)}, f32[44,256]{1,0:T(8,128)S(1)}, u32[]{:S(2)}, u32[]{:S(2)}) collective-permute-start(f32[44,256]{1,0:T(8,128)S(1)} %slice.50), channel_id=1, source_target_pairs={{0,1},{1,0},{2,3},{3,2},{4,5},{5,4},{6,7},{7,6},{8,9},{9,8},{10,11... | collective-permute-start | bytes 135176 | tf_op jit(solution)/shard_map/ppermute | solution.py:535
  293.9 17.4 %collective-permute-start.48 = (f32[1,128,1024]{2,1,0:T(8,128)}, f32[1,128,1024]{2,1,0:T(8,128)S(1)}, u32[]{:S(2)}, u32[]{:S(2)}) collective-permute-start(f32[1,128,1024]{2,1,0:T(8,128)} %get-tuple-element.132), channel_id=1, source_target_pairs={{0,16},{4,20},{8,24},{12,28},{16,0},{20,4},{24,8},{28,12},{1,17},{... | collective-permute-start | bytes 1572872 | tf_op jit(solution)/shard_map/ppermute | solution.py:535
  295.5 15.8 %collective-permute-start.49 = (f32[1,128,1024]{2,1,0:T(8,128)}, f32[1,128,1024]{2,1,0:T(8,128)S(1)}, u32[]{:S(2)}, u32[]{:S(2)}) collective-permute-start(f32[1,128,1024]{2,1,0:T(8,128)} %get-tuple-element.134), channel_id=1, source_target_pairs={{0,8},{4,12},{8,0},{12,4},{16,24},{20,28},{24,16},{28,20},{1,9},{5... | collective-permute-start | bytes 1572872 | tf_op jit(solution)/shard_map/ppermute | solution.py:535
  303.7 5.9 %collective-permute-start.43 = (f32[128,288]{1,0:T(8,128)}, f32[128,288]{1,0:T(8,128)S(1)}, u32[]{:S(2)}, u32[]{:S(2)}) collective-permute-start(f32[128,288]{1,0:T(8,128)} %collective-permute-done.42), channel_id=1, source_target_pairs={{0,1},{1,0},{2,3},{3,2},{4,5},{5,4},{6,7},{7,6},{8,9},{9,8},{10,11... | collective-permute-start | bytes 442376 | tf_op jit(solution)/shard_map/ppermute | solution.py:535
  (33 other events, 545.4 us)
